TPU v7x, 32 devices: a whole 2x2x4 slice. The times are simulated.
32 devices in a mesh: dp: 4 (over y, x), fsdp: 8 (over z, core).
Axes of the slice: x: 2, y: 2, z: 4, core: 2. Of those that a mesh axis runs over, the one named last changes fastest.
Arguments:
- tokens: bfloat16 [16384, 768], P(('dp', 'fsdp')), may hold values from -6 to 6
- in_weight: bfloat16 [768, 2304], P('fsdp'), may hold values from -0.21875 to 0.21875
- in_bias: bfloat16 [1536], P('fsdp'), may hold values from -1.75 to 1.75
- mix_weight: bfloat16 [768, 768], P('fsdp'), may hold values from -2.5 to 2.5
- mix_bias: bfloat16 [768], P('fsdp'), may hold values from -1.75 to 1.75
- first_gain: bfloat16 [768], P('fsdp'), may hold values from 0.5 to 1.5
- first_shift: bfloat16 [768], P('fsdp'), may hold values from -1.75 to 1.75
- up_weight: bfloat16 [768, 3072], P('fsdp'), may hold values from -0.21875 to 0.21875
- up_bias: bfloat16 [3072], P('fsdp'), may hold values from -3 to 3
- down_weight: bfloat16 [3072, 768], P('fsdp'), may hold values from -0.109375 to 0.109375
- down_bias: bfloat16 [768], P('fsdp'), may hold values from -1.75 to 1.75
- second_gain: bfloat16 [768], P('fsdp'), may hold values from 0.5 to 1.5
- second_shift: bfloat16 [768], P('fsdp'), may hold values from -1.75 to 1.75
- pool_weight: bfloat16 [768, 768], P('fsdp'), may hold values from -0.21875 to 0.21875
- pool_bias: bfloat16 [768], P('fsdp'), may hold values from -3 to 3
- class_weight: bfloat16 [768, 3], P('fsdp'), may hold values from -0.625 to 0.625
- class_bias: bfloat16 [3], replicated, may hold values from -3 to 3
- lengths: int32 [32], P(('dp', 'fsdp')), may hold values from 1 to 512, 10240 in all
- labels: int32 [32], P(('dp', 'fsdp')), may hold values from 0 to 2
- cotangent: bfloat16 [16384, 768], P(('dp', 'fsdp')), may hold values from -6 to 6
Outputs:
- layer_out: bfloat16 [16384, 768], P(('dp', 'fsdp'))
- input_grad: float32 [16384, 768], P(('dp', 'fsdp'))
- grad_in_weight: float32 [768, 2304], P('fsdp')
- grad_in_bias: float32 [1536], P('fsdp')
- grad_mix_weight: float32 [768, 768], P('fsdp')
- grad_mix_bias: float32 [768], P('fsdp')
- grad_first_gain: float32 [768], P('fsdp')
- grad_first_shift: float32 [768], P('fsdp')
- grad_up_weight: float32 [768, 3072], P('fsdp')
- grad_up_bias: float32 [3072], P('fsdp')
- grad_down_weight: float32 [3072, 768], P('fsdp')
- grad_down_bias: float32 [768], P('fsdp')
- grad_second_gain: float32 [768], P('fsdp')
- grad_second_shift: float32 [768], P('fsdp')
- grad_pool_weight: float32 [768, 768], P('fsdp')
- grad_pool_bias: float32 [768], P('fsdp')
- grad_class_weight: float32 [768, 3], P('fsdp')
- grad_class_bias: float32 [3], replicated
Inputs may be any that keep to these rules, and one draw needn't show every extreme that they name: `lengths`: tokens of a sequence at positions at or past its length are padding; some sequence has exactly 512.
All inputs are finite; a program needn't handle non-finite values. No bound on the sum of `lengths` on one device may be relied on, other than what follows from the above.
Results may differ from a plain program's by a relative error of at most 0.017.
Values may be sent and summed in bfloat16 or wider, within the bound.
A program may use at most 128 MiB of HBM per device.

v0:
```python
from functools import partial
import math

import jax
import jax.numpy as jnp
from jax import lax
from jax.sharding import PartitionSpec as P

H = 12
DH = 64


EPSILON = 1e-06


def norm_fore(vector, norm_gain, norm_shift):
    average = jnp.mean(vector, axis=-1, keepdims=True)
    centered = vector - average
    inverse = lax.rsqrt(jnp.mean(centered * centered, axis=-1, keepdims=True) + EPSILON)
    normed = centered * inverse
    return (normed * norm_gain + norm_shift, normed, inverse)


def norm_back(gradient, normed, inverse, norm_gain):
    scaled = gradient * norm_gain
    inner_mean = jnp.mean(scaled, axis=-1, keepdims=True)
    cross_mean = jnp.mean(scaled * normed, axis=-1, keepdims=True)
    input_part = inverse * (scaled - inner_mean - normed * cross_mean)
    return (input_part, jnp.sum(gradient * normed, axis=0), jnp.sum(gradient, axis=0))


def column_sums(matrix):
    return jnp.sum(matrix.astype(jnp.float32), axis=0)


def body(
    tokens,
    in_weight,
    in_bias,
    mix_weight,
    mix_bias,
    first_gain,
    first_shift,
    up_weight,
    up_bias,
    down_weight,
    down_bias,
    second_gain,
    second_shift,
    pool_weight,
    pool_bias,
    class_weight,
    class_bias,
    lengths,
    labels,
    cotangent,
):
    gathered = (
        lax.all_gather(in_weight, "fsdp", axis=0, tiled=True),
        lax.all_gather(in_bias, "fsdp", axis=0, tiled=True),
        lax.all_gather(mix_weight, "fsdp", axis=0, tiled=True),
        lax.all_gather(mix_bias, "fsdp", axis=0, tiled=True),
        lax.all_gather(first_gain, "fsdp", axis=0, tiled=True),
        lax.all_gather(first_shift, "fsdp", axis=0, tiled=True),
        lax.all_gather(up_weight, "fsdp", axis=0, tiled=True),
        lax.all_gather(up_bias, "fsdp", axis=0, tiled=True),
        lax.all_gather(down_weight, "fsdp", axis=0, tiled=True),
        lax.all_gather(down_bias, "fsdp", axis=0, tiled=True),
        lax.all_gather(second_gain, "fsdp", axis=0, tiled=True),
        lax.all_gather(second_shift, "fsdp", axis=0, tiled=True),
        lax.all_gather(pool_weight, "fsdp", axis=0, tiled=True),
        lax.all_gather(pool_bias, "fsdp", axis=0, tiled=True),
        lax.all_gather(class_weight, "fsdp", axis=0, tiled=True),
    )
    (
        whole_in,
        bias_in,
        whole_mix,
        bias_mix,
        gain_one,
        shift_one,
        whole_up,
        bias_up,
        whole_down,
        bias_down,
        gain_two,
        shift_two,
        whole_pool,
        bias_pool,
        whole_class,
    ) = gathered
    token_rows = tokens.shape[0]
    seq_count = lengths.shape[0]
    seq_len = token_rows // seq_count
    model_width = whole_mix.shape[0]
    score_scale = 1.0 / math.sqrt(DH)
    positions = jnp.arange(seq_len)
    projected = jnp.dot(tokens, whole_in, preferred_element_type=jnp.float32)
    in_bias_f = bias_in.astype(jnp.float32)
    head_shape = (seq_count, seq_len, H, DH)
    queries = (
        (projected[:, :model_width] + in_bias_f[:model_width])
        .astype(jnp.bfloat16)
        .reshape(head_shape)
    )
    keys_all = projected[:, model_width : 2 * model_width].astype(jnp.bfloat16).reshape(head_shape)
    values_all = (
        (projected[:, 2 * model_width :] + in_bias_f[model_width:])
        .astype(jnp.bfloat16)
        .reshape(head_shape)
    )

    def scores_of(query_blk, key_blk, length):
        raw_scores = (
            jnp.einsum("qhd,khd->hqk", query_blk, key_blk, preferred_element_type=jnp.float32)
            * score_scale
        )
        return jnp.where(positions[None, None, :] < length, raw_scores, -1e30)

    def attend_fore(block_items):
        query_blk, key_blk, value_blk, length = block_items
        scores = scores_of(query_blk, key_blk, length)
        highest = jnp.max(scores, axis=-1, keepdims=True)
        raw_weights = jnp.exp(scores - highest)
        totals = jnp.sum(raw_weights, axis=-1, keepdims=True)
        softmaxed = (raw_weights / totals).astype(jnp.bfloat16)
        mixed_values = jnp.einsum(
            "hqk,khd->qhd", softmaxed, value_blk, preferred_element_type=jnp.float32
        )
        return (mixed_values, (highest + jnp.log(totals))[..., 0])

    attended, logsum = lax.map(attend_fore, (queries, keys_all, values_all, lengths))
    attn_low = attended.reshape(token_rows, model_width).astype(jnp.bfloat16)
    branch = jnp.dot(attn_low, whole_mix, preferred_element_type=jnp.float32) + bias_mix.astype(
        jnp.float32
    )
    first_norm, unit_one, inverse_one = norm_fore(
        tokens.astype(jnp.float32) + branch,
        gain_one.astype(jnp.float32),
        shift_one.astype(jnp.float32),
    )
    first_low = first_norm.astype(jnp.bfloat16)
    pre_act = jnp.dot(first_low, whole_up, preferred_element_type=jnp.float32) + bias_up.astype(
        jnp.float32
    )
    activated, gelu_pull = jax.vjp(partial(jax.nn.gelu, approximate=False), pre_act)
    act_low = activated.astype(jnp.bfloat16)
    ffn_out = jnp.dot(act_low, whole_down, preferred_element_type=jnp.float32) + bias_down.astype(
        jnp.float32
    )
    result, unit_two, inverse_two = norm_fore(
        first_norm + ffn_out, gain_two.astype(jnp.float32), shift_two.astype(jnp.float32)
    )
    head_rows = result.reshape(seq_count, seq_len, model_width)[:, 0, :].astype(jnp.bfloat16)
    pooled = jnp.tanh(
        jnp.dot(head_rows, whole_pool, preferred_element_type=jnp.float32)
        + bias_pool.astype(jnp.float32)
    )
    pooled_low = pooled.astype(jnp.bfloat16)
    logits = jnp.dot(
        pooled_low, whole_class, preferred_element_type=jnp.float32
    ) + class_bias.astype(jnp.float32)
    back_in, back_mix, back_gain_one, back_up, back_down, back_gain_two, back_pool, back_class = (
        lax.all_gather(in_weight, "fsdp", axis=0, tiled=True),
        lax.all_gather(mix_weight, "fsdp", axis=0, tiled=True),
        lax.all_gather(first_gain, "fsdp", axis=0, tiled=True),
        lax.all_gather(up_weight, "fsdp", axis=0, tiled=True),
        lax.all_gather(down_weight, "fsdp", axis=0, tiled=True),
        lax.all_gather(second_gain, "fsdp", axis=0, tiled=True),
        lax.all_gather(pool_weight, "fsdp", axis=0, tiled=True),
        lax.all_gather(class_weight, "fsdp", axis=0, tiled=True),
    )
    onehot = (labels[:, None] == jnp.arange(logits.shape[1])[None, :]).astype(jnp.float32)
    grad_logits = (jax.nn.softmax(logits, axis=-1) - onehot).astype(jnp.bfloat16)
    grad_class_weight = jnp.dot(pooled_low.T, grad_logits, preferred_element_type=jnp.float32)
    grad_class_bias = column_sums(grad_logits)
    grad_pool_pre = (
        jnp.dot(grad_logits, back_class.T, preferred_element_type=jnp.float32)
        * (1.0 - pooled * pooled)
    ).astype(jnp.bfloat16)
    grad_pool_weight = jnp.dot(head_rows.T, grad_pool_pre, preferred_element_type=jnp.float32)
    grad_pool_bias = column_sums(grad_pool_pre)
    grad_head_rows = jnp.dot(grad_pool_pre, back_pool.T, preferred_element_type=jnp.float32)
    live_mask = (positions[None, :] < lengths[:, None]).astype(jnp.float32)
    grad_result = (
        cotangent.astype(jnp.float32).reshape(seq_count, seq_len, model_width)
        * live_mask[:, :, None]
    )
    grad_result = grad_result.at[:, 0, :].add(grad_head_rows).reshape(token_rows, model_width)
    grad_sum_two, grad_second_gain, grad_second_shift = norm_back(
        grad_result, unit_two, inverse_two, back_gain_two.astype(jnp.float32)
    )
    grad_ffn = grad_sum_two.astype(jnp.bfloat16)
    grad_down_weight = jnp.dot(act_low.T, grad_ffn, preferred_element_type=jnp.float32)
    grad_down_bias = column_sums(grad_ffn)
    grad_pre = gelu_pull(jnp.dot(grad_ffn, back_down.T, preferred_element_type=jnp.float32))[
        0
    ].astype(jnp.bfloat16)
    grad_up_weight = jnp.dot(first_low.T, grad_pre, preferred_element_type=jnp.float32)
    grad_up_bias = column_sums(grad_pre)
    grad_first_norm = grad_sum_two + jnp.dot(
        grad_pre, back_up.T, preferred_element_type=jnp.float32
    )
    grad_sum_one, grad_first_gain, grad_first_shift = norm_back(
        grad_first_norm, unit_one, inverse_one, back_gain_one.astype(jnp.float32)
    )
    grad_branch = grad_sum_one.astype(jnp.bfloat16)
    grad_mix_weight = jnp.dot(attn_low.T, grad_branch, preferred_element_type=jnp.float32)
    grad_mix_bias = column_sums(grad_branch)
    grad_attended = (
        jnp.dot(grad_branch, back_mix.T, preferred_element_type=jnp.float32)
        .astype(jnp.bfloat16)
        .reshape(head_shape)
    )

    def attend_back(block_items):
        query_blk, key_blk, value_blk, length, lse_blk, grad_blk = block_items
        softmaxed = jnp.exp(scores_of(query_blk, key_blk, length) - lse_blk[..., None])
        grad_value = jnp.einsum(
            "hqk,qhd->khd",
            softmaxed.astype(jnp.bfloat16),
            grad_blk,
            preferred_element_type=jnp.float32,
        )
        grad_soft = jnp.einsum(
            "qhd,khd->hqk", grad_blk, value_blk, preferred_element_type=jnp.float32
        )
        grad_scores = (
            softmaxed * (grad_soft - jnp.sum(softmaxed * grad_soft, axis=-1, keepdims=True))
        ).astype(jnp.bfloat16)
        grad_query = (
            jnp.einsum("hqk,khd->qhd", grad_scores, key_blk, preferred_element_type=jnp.float32)
            * score_scale
        )
        grad_key = (
            jnp.einsum("hqk,qhd->khd", grad_scores, query_blk, preferred_element_type=jnp.float32)
            * score_scale
        )
        return (grad_query, grad_key, grad_value)

    grad_queries, grad_keys, grad_values = lax.map(
        attend_back, (queries, keys_all, values_all, lengths, logsum, grad_attended)
    )
    grad_proj = jnp.concatenate(
        [
            grad_queries.reshape(token_rows, model_width),
            grad_keys.reshape(token_rows, model_width),
            grad_values.reshape(token_rows, model_width),
        ],
        axis=1,
    ).astype(jnp.bfloat16)
    grad_in_weight = jnp.dot(tokens.T, grad_proj, preferred_element_type=jnp.float32)
    proj_sums = column_sums(grad_proj)
    grad_in_bias = jnp.concatenate([proj_sums[:model_width], proj_sums[2 * model_width :]])
    input_grad = grad_sum_one + jnp.dot(grad_proj, back_in.T, preferred_element_type=jnp.float32)
    gradients = (
        grad_in_weight,
        grad_in_bias,
        grad_mix_weight,
        grad_mix_bias,
        grad_first_gain,
        grad_first_shift,
        grad_up_weight,
        grad_up_bias,
        grad_down_weight,
        grad_down_bias,
        grad_second_gain,
        grad_second_shift,
        grad_pool_weight,
        grad_pool_bias,
        grad_class_weight,
    )
    shard_sums = (
        lax.psum_scatter(gradients[0], "fsdp", scatter_dimension=0, tiled=True),
        lax.psum_scatter(gradients[1], "fsdp", scatter_dimension=0, tiled=True),
        lax.psum_scatter(gradients[2], "fsdp", scatter_dimension=0, tiled=True),
        lax.psum_scatter(gradients[3], "fsdp", scatter_dimension=0, tiled=True),
        lax.psum_scatter(gradients[4], "fsdp", scatter_dimension=0, tiled=True),
        lax.psum_scatter(gradients[5], "fsdp", scatter_dimension=0, tiled=True),
        lax.psum_scatter(gradients[6], "fsdp", scatter_dimension=0, tiled=True),
        lax.psum_scatter(gradients[7], "fsdp", scatter_dimension=0, tiled=True),
        lax.psum_scatter(gradients[8], "fsdp", scatter_dimension=0, tiled=True),
        lax.psum_scatter(gradients[9], "fsdp", scatter_dimension=0, tiled=True),
        lax.psum_scatter(gradients[10], "fsdp", scatter_dimension=0, tiled=True),
        lax.psum_scatter(gradients[11], "fsdp", scatter_dimension=0, tiled=True),
        lax.psum_scatter(gradients[12], "fsdp", scatter_dimension=0, tiled=True),
        lax.psum_scatter(gradients[13], "fsdp", scatter_dimension=0, tiled=True),
        lax.psum_scatter(gradients[14], "fsdp", scatter_dimension=0, tiled=True),
    )
    summed = (
        lax.psum(shard_sums[0].astype(jnp.bfloat16), "dp").astype(jnp.float32),
        lax.psum(shard_sums[1].astype(jnp.bfloat16), "dp").astype(jnp.float32),
        lax.psum(shard_sums[2].astype(jnp.bfloat16), "dp").astype(jnp.float32),
        lax.psum(shard_sums[3].astype(jnp.bfloat16), "dp").astype(jnp.float32),
        lax.psum(shard_sums[4].astype(jnp.bfloat16), "dp").astype(jnp.float32),
        lax.psum(shard_sums[5].astype(jnp.bfloat16), "dp").astype(jnp.float32),
        lax.psum(shard_sums[6].astype(jnp.bfloat16), "dp").astype(jnp.float32),
        lax.psum(shard_sums[7].astype(jnp.bfloat16), "dp").astype(jnp.float32),
        lax.psum(shard_sums[8].astype(jnp.bfloat16), "dp").astype(jnp.float32),
        lax.psum(shard_sums[9].astype(jnp.bfloat16), "dp").astype(jnp.float32),
        lax.psum(shard_sums[10].astype(jnp.bfloat16), "dp").astype(jnp.float32),
        lax.psum(shard_sums[11].astype(jnp.bfloat16), "dp").astype(jnp.float32),
        lax.psum(shard_sums[12].astype(jnp.bfloat16), "dp").astype(jnp.float32),
        lax.psum(shard_sums[13].astype(jnp.bfloat16), "dp").astype(jnp.float32),
        lax.psum(shard_sums[14].astype(jnp.bfloat16), "dp").astype(jnp.float32),
    )
    bias_total = lax.psum(grad_class_bias, ("dp", "fsdp"))
    return (
        result.astype(jnp.bfloat16),
        input_grad,
        summed[0],
        summed[1],
        summed[2],
        summed[3],
        summed[4],
        summed[5],
        summed[6],
        summed[7],
        summed[8],
        summed[9],
        summed[10],
        summed[11],
        summed[12],
        summed[13],
        summed[14],
        bias_total,
    )


def solution(mesh):
    in_specs = (
        P(("dp", "fsdp"), None),
        P("fsdp", None),
        P("fsdp"),
        P("fsdp", None),
        P("fsdp"),
        P("fsdp"),
        P("fsdp"),
        P("fsdp", None),
        P("fsdp"),
        P("fsdp", None),
        P("fsdp"),
        P("fsdp"),
        P("fsdp"),
        P("fsdp", None),
        P("fsdp"),
        P("fsdp", None),
        P(),
        P(("dp", "fsdp")),
        P(("dp", "fsdp")),
        P(("dp", "fsdp"), None),
    )
    out_specs = (
        P(("dp", "fsdp"), None),
        P(("dp", "fsdp"), None),
        P("fsdp", None),
        P("fsdp"),
        P("fsdp", None),
        P("fsdp"),
        P("fsdp"),
        P("fsdp"),
        P("fsdp", None),
        P("fsdp"),
        P("fsdp", None),
        P("fsdp"),
        P("fsdp"),
        P("fsdp"),
        P("fsdp", None),
        P("fsdp"),
        P("fsdp", None),
        P(),
    )
    return jax.shard_map(body, mesh=mesh, in_specs=in_specs, out_specs=out_specs, check_vma=False)
```

profile of v0, /device:TPU:8, one launch (start us, length us, event | category | flops | bytes accessed | tf_op | source)
XLA Modules:
  0.0 703.2 jit_solution(4559196718657243152)
XLA Ops:
  22.0 27.0 %all-reduce.18 = (bf16[1536]{0:T(1024)(128)(2,1)S(1)}, bf16[768]{0:T(1024)(128)(2,1)S(1)}, bf16[768]{0:T(1024)(128)(2,1)S(1)}, bf16[768]{0:T(1024)(128)(2,1)S(1)...) all-reduce(bf16[1536]{0:T(1024)(128)(2,1)S(1)} %dynamic-update-slic, ...), channel_id=1, replica_groups=mesh['dp'=4,'fsdp'=8] {'fsdp'}, use_global_device_ids=true, to_apply=%add | all-reduce | flops 6912 | bytes 27648
  49.0 12.7 %all-gather.1 = bf16[8,96,3]{1,2,0:T(4,128)(2,1)S(1)} all-gather(bf16[1,96,3]{1,2,0:T(4,128)(2,1)} %bitcast.99), channel_id=1, replica_groups=mesh['dp'=4,'fsdp'=8] {'fsdp'}, dimensions={0}, use_global_device_ids=true | all-gather | bytes 5184 | tf_op jit(solution)/shard_map/all_gather | solution.py:73
  61.9 11.7 %all-gather = bf16[8,1,384]{2,1,0:T(2,128)(2,1)S(1)} all-gather(bf16[1,1,384]{2,1,0:T(2,128)(2,1)S(1)} %reshape.287), channel_id=1, replica_groups=mesh['dp'=4,'fsdp'=8] {'fsdp'}, dimensions={0}, use_global_device_ids=true | all-gather | bytes 6912 | tf_op jit(solution)/shard_map/all_gather | solution.py:66
  75.0 4.0 fusion.52
  81.5 1.7 copy.63
  83.2 2.6 copy.61
  85.8 3.0 fusion.48
  88.8 1.8 fusion
  90.7 2.7 copy-done
  93.4 3.4 fusion.17
  96.8 2.7 fusion.49
  99.8 27.6 %all-gather.12.cloned.1.call-done = bf16[768,3072]{1,0:T(8,128)(2,1)} async-done(((bf16[96,3072]{1,0:T(8,128)(2,1)}), bf16[768,3072]{1,0:T(8,128)(2,1)}) %all-gather.12.cloned.1.call-update) | async-done | bytes 4718608 | tf_op jit(solution)/shard_map/all_gather | solution.py:65
  127.3 19.7 %multiply_convert_fusion.1 = (bf16[512,3072]{1,0:T(8,128)(2,1)}, f32[512,3072]{1,0:T(8,128)}, f32[512,3072]{1,0:T(8,128)}) fusion(f32[3072]{0:T(1024)S(1)} %bitcast.97, bf16[768,3072]{1,0:T(8,128)(2,1)} %all-gather.12.cloned.1.call-done, f32[512,768]{1,0:T(8,128)S(1)} %get-tuple-element.205, f32[768]{0:T(1024)S(1)} %convert_element_type.241, ...), kind=kOutput, calls=%fused_computation.14 | convolution fusion | flops 2521694208 | bytes 22042624 | tf_op jit(solution)/shard_map/dot_general | solution.py:143
  147.0 31.8 %all-gather.14.cloned.1.call-done = bf16[3072,768]{1,0:T(8,128)(2,1)} async-done(((bf16[384,768]{1,0:T(8,128)(2,1)}), bf16[3072,768]{1,0:T(8,128)(2,1)}) %all-gather.14.cloned.1.call-update) | async-done | bytes 4718608 | tf_op jit(solution)/shard_map/all_gather | solution.py:67
  178.8 6.5 fusion.50
  186.8 16.4 %all-gather.16.cloned.1.call-done = bf16[768,768]{1,0:T(8,128)(2,1)} async-done(((bf16[96,768]{1,0:T(8,128)(2,1)}), bf16[768,768]{1,0:T(8,128)(2,1)}) %all-gather.16.cloned.1.call-update) | async-done | bytes 1179664 | tf_op jit(solution)/shard_map/all_gather | solution.py:71
  208.3 1.7 convolution_reduce_fusion
  212.4 9.7 %convert_reduce_fusion = (f32[3072]{0:T(1024)S(1)}, bf16[512,3072]{1,0:T(8,128)(2,1)S(1)}) fusion(f32[512,3072]{1,0:T(8,128)} %get-tuple-element.192, bf16[3072,768]{1,0:T(8,128)(2,1)} %all-gather.14.cloned.1.call-done, f32[512,768]{1,0:T(8,128)S(1)} %get-tuple-element.186, f32[512,3072]{1,0:T(8,128)} %get-tuple-element.206, f32[3072]{0:T(1024)S(1)} %bitcast.98), kind=kOutput, calls=%fused_computation.11 | convolution fusion | flops 2443047936 | bytes 22044672 | tf_op jit(solution)/shard_map/dot_general | solution.py:196
  222.1 3.1 multiply_reduce_fusion.2
  226.4 2.2 fusion.25
  229.4 1.6 broadcast_multiply_fusion
  231.2 3.0 convolution_convert_fusion
  235.7 10.9 %multiply_reduce_fusion = (f32[12,512]{1,0:T(8,128)S(1)}, f32[12,512,512]{1,2,0:T(8,128)}) fusion(f32[12,512,512]{1,2,0:T(8,128)} %copy-done, f32[12,512]{1,0:T(8,128)S(1)} %log_add_fusion, bf16[512,12,64]{0,2,1:T(8,128)(2,1)S(1)} %bitcast.80, bf16[512,12,64]{0,2,1:T(8,128)(2,1)} %bitcast.87), kind=kOutput, calls=%fused_computation.1 | convolution fusion | flops 412084224 | bytes 26787840 | tf_op jit(solution)/shard_map/while/body/eval_jaxpr/qhd,khd->hqk/dot_general | solution.py:225
  248.7 7.0 multiply_convert_fusion
  255.7 2.0 multiply_convert_fusion.2
  258.8 2.0 fusion.14
  261.8 4.9 convolution_bitcast_fusion
  266.7 8.0 %copy.75 = f32[768,2304]{1,0:T(8,128)} copy(f32[768,2304]{0,1:T(8,128)} %convolution_bitcast_fusion) | data formatting | bytes 14155776
  274.8 7.2 %fusion.36 = f32[768,3072]{1,0:T(8,128)} fusion(bf16[512,3072]{1,0:T(8,128)(2,1)} %copy-done.20, f32[512,768]{1,0:T(8,128)S(1)} %copy-done.8, f32[768]{0:T(1024)S(1)} %convert_element_type.241, f32[768]{0:T(1024)S(1)} %convert_element_type.240, f32[512]{0:T(512)S(1)} %add_rsqrt_fusion.1, f32[512]{0:T(512)S(1)} %broadcast_multiply_fusion.7), kind=kOutput, calls=%fused_computation.114 | convolution fusion | flops 2417885184 | bytes 14166016 | tf_op jit(solution)/shard_map/dot_general | solution.py:199
  283.5 8.2 %fusion.28 = f32[3072,768]{1,0:T(8,128)} fusion(bf16[512,3072]{1,0:T(8,128)(2,1)} %get-tuple-element.191, f32[512,768]{1,0:T(8,128)S(1)} %copy-done.6), kind=kOutput, calls=%fused_computation.108 | convolution fusion | flops 2416312320 | bytes 14155776 | tf_op jit(solution)/shard_map/dot_general | solution.py:194
  292.9 1.6 convert_element_type.270
  294.5 5.5 reduce-scatter.17.cloned.1.call-done
  300.1 1.6 convert_element_type.293
  301.7 77.9 %reduce-scatter.19.cloned.1.call-done = f32[96,2304]{1,0:T(8,128)} async-done(((f32[768,2304]{1,0:T(8,128)}), f32[96,2304]{1,0:T(8,128)}) %reduce-scatter.19.cloned.1.call-update) | async-done | bytes 884752
  379.6 2.2 copy.76
  381.8 98.0 %reduce-scatter.13.cloned.1.call-done = f32[96,3072]{1,0:T(8,128)} async-done(((f32[768,3072]{1,0:T(8,128)}), f32[96,3072]{1,0:T(8,128)}) %reduce-scatter.13.cloned.1.call-update) | async-done | bytes 1179664 | tf_op jit(solution)/shard_map/reduce_scatter | solution.py:280
  479.8 2.2 convert_element_type.279
  482.0 97.9 %reduce-scatter.15.cloned.1.call-done = f32[384,768]{1,0:T(8,128)} async-done(((f32[3072,768]{1,0:T(8,128)}), f32[384,768]{1,0:T(8,128)}) %reduce-scatter.15.cloned.1.call-update) | async-done | bytes 1179664 | tf_op jit(solution)/shard_map/reduce_scatter | solution.py:282
  579.9 2.2 convert_element_type.284
  584.0 42.1 %psum.127 = f32[3]{0:T(128)} all-reduce(bf16[3]{0:T(256)(128)(2,1)S(1)} %get-tuple-element.184), channel_id=1, replica_groups=mesh['dp'=4,'fsdp'=8] {'dp','fsdp'}, use_global_device_ids=true, to_apply=%region_51.52 | all-reduce | flops 3 | bytes 18 | tf_op jit(solution)/shard_map/psum | solution.py:307
  627.7 22.6 %all-reduce.17 = (bf16[1536]{0:T(1024)(128)(2,1)S(1)}, bf16[768]{0:T(1024)(128)(2,1)S(1)}, bf16[768]{0:T(1024)(128)(2,1)S(1)}, bf16[768]{0:T(1024)(128)(2,1)S(1)...) all-reduce(f32[1536]{0:T(1024)S(1)} %pad_maximum_fusion.1, ...), channel_id=3, replica_groups=mesh['dp'=4,'fsdp'=8] {'fsdp'}, use_global_device_ids=true, to_apply=%region_16.17.clone | all-reduce | flops 9984 | bytes 58368
  651.0 5.5 convolution_add_fusion
  657.3 10.3 %all-reduce.19 = (bf16[192]{0:T(256)(128)(2,1)S(1)}, bf16[96]{0:T(256)(128)(2,1)S(1)}, bf16[96]{0:T(256)(128)(2,1)S(1)}, bf16[96]{0:T(256)(128)(2,1)S(1)}, bf16[...) all-reduce(bf16[192]{0:T(256)(128)(2,1)S(1)} %dynamic-slice.44, ...), channel_id=1, replica_groups=mesh['dp'=4,'fsdp'=8] {'dp'}, use_global_device_ids=true, to_apply=%region_17.18 | all-reduce | flops 1536 | bytes 6144 | tf_op jit(solution)/shard_map/psum | solution.py:292
  673.0 14.3 %all-reduce.23.cloned.1.call-done = (bf16[96,2304]{0,1:T(8,128)(2,1)}, bf16[96,768]{1,0:T(8,128)(2,1)}, bf16[96,3072]{1,0:T(8,128)(2,1)}, bf16[384,768]{1,0:T(8,128)(2,1)}, bf16[96,768]{1,0:T(8,128)(2,1)}) async-done(((bf16[96,2304]{0,1:T(8,128)(2,1)}, bf16[96,768]{1,0:T(8,128)(2,1)}, bf16[96,3072]{1,0:T(8,128)(2,1)}, bf16[384,768]{1,0:T(8,128)(2,1)}, bf16[96,768]{1,0:T(8,128)(2,1)}), ...) | async-done | bytes 1916944 | tf_op jit(solution)/shard_map/psum | solution.py:291
  687.3 2.3 copy.70
  689.5 1.6 convert_element_type.271
  691.2 1.6 convert_element_type.294
  692.8 2.2 convert_element_type.280
  (172 shorter events, 44.9 us)
Async XLA Ops:
  7.2 67.8 %copy-start.17 = (bf16[512,768]{1,0:T(8,128)(2,1)S(1)}, bf16[512,768]{1,0:T(8,128)(2,1)}, u32[]{:S(2)}) copy-start(bf16[512,768]{1,0:T(8,128)(2,1)} %param.22) | copy-start | bytes 2359300
  7.2 67.8 %all-gather.8.cloned.1.call-start = ((), (), s32[]{:S(2)}) async-start(), calls=%async_computation.6 | async-start | bytes 3981312 | tf_op jit(solution)/shard_map/all_gather | solution.py:59
  7.9 88.9 %all-gather.10.cloned.1.call-start = ((), (), s32[]{:S(2)}) async-start(), calls=%async_computation.7 | async-start | bytes 1327104 | tf_op jit(solution)/shard_map/all_gather | solution.py:61
  8.7 118.7 %all-gather.12.cloned.1.call-start = ((), (), s32[]{:S(2)}) async-start(), calls=%async_computation.8 | async-start | bytes 5308416 | tf_op jit(solution)/shard_map/all_gather | solution.py:65
  9.4 169.4 %all-gather.14.cloned.1.call-start = ((), (), s32[]{:S(2)}) async-start(), calls=%async_computation.9 | async-start | bytes 5308416 | tf_op jit(solution)/shard_map/all_gather | solution.py:67
  10.0 193.3 %all-gather.16.cloned.1.call-start = ((), (), s32[]{:S(2)}) async-start(), calls=%async_computation.10 | async-start | bytes 1327104 | tf_op jit(solution)/shard_map/all_gather | solution.py:71
  10.6 282.3 %reduce-scatter.11.cloned.1.call-start = ((), (), s32[]{:S(2)}) async-start(), calls=%async_computation.11 | async-start | bytes 2654208 | tf_op jit(solution)/shard_map/reduce_scatter | solution.py:276
  81.4 7.4 %copy-start.3 = (bf16[512,768]{0,1:T(8,128)(2,1)}, bf16[512,768]{0,1:T(8,128)(2,1)S(1)}, u32[]{:S(2)}) copy-start(bf16[512,768]{0,1:T(8,128)(2,1)S(1)} %copy.62) | copy-start | bytes 2359300
  83.2 5.7 copy-start.1
  88.8 4.6 copy-start
  88.8 4.6 copy-start.11
  99.4 47.6 %copy-start.7 = (f32[512,768]{1,0:T(8,128)}, f32[512,768]{1,0:T(8,128)S(1)}, u32[]{:S(2)}) copy-start(f32[512,768]{1,0:T(8,128)S(1)} %get-tuple-element.205) | copy-start | bytes 4718596
  185.3 19.6 %copy-start.19 = (bf16[3]{0:T(256)(128)(2,1)S(1)}, bf16[3]{0:T(256)(128)(2,1)}, u32[]{:S(2)}) copy-start(bf16[3]{0:T(256)(128)(2,1)} %param.38) | copy-start | bytes 22
  210.9 11.2 %slice-start.3 = ((s8[4718592]{0:T(1024)(128)(4,1)}), s8[4194304]{0:T(1024)(128)(4,1)S(1)}, s32[]{:S(2)}) async-start(s8[4718592]{0:T(1024)(128)(4,1)} %bitcast.100), calls=%async_computation.21 | async-start | bytes 8388608
  212.4 9.7 %copy-start.5 = (f32[512,768]{1,0:T(8,128)}, f32[512,768]{1,0:T(8,128)S(1)}, u32[]{:S(2)}) copy-start(f32[512,768]{1,0:T(8,128)S(1)} %get-tuple-element.186) | copy-start | bytes 4718596
  212.4 9.7 %copy-start.8 = (f32[512,768]{1,0:T(8,128)S(1)}, f32[512,768]{1,0:T(8,128)}, u32[]{:S(2)}) copy-start(f32[512,768]{1,0:T(8,128)} %copy-done.7) | copy-start | bytes 4718596
  212.4 9.7 %slice-start.4 = ((s8[4718592]{0:T(1024)(128)(4,1)}), s8[524288]{0:T(1024)(128)(4,1)S(1)}, s32[]{:S(2)}) async-start(s8[4718592]{0:T(1024)(128)(4,1)} %bitcast.100), calls=%async_computation.22 | async-start | bytes 1048576
  222.1 3.2 copy-start.20
  225.3 1.1 copy-start.15
  225.8 5.4 copy-start.9
  228.6 71.4 %reduce-scatter.17.cloned.1.call-start = ((), (), s32[]{:S(2)}) async-start(), calls=%async_computation.14 | async-start | bytes 2654208 | tf_op jit(solution)/shard_map/reduce_scatter | solution.py:286
  231.1 148.5 %reduce-scatter.19.cloned.1.call-start = ((), (), s32[]{:S(2)}) async-start(), calls=%async_computation.15 | async-start | bytes 7962624
  235.6 10.9 %slice-start = ((s8[12582912]{0:T(1024)(128)(4,1)}), s8[4194304]{0:T(1024)(128)(4,1)S(1)}, s32[]{:S(2)}) async-start(s8[12582912]{0:T(1024)(128)(4,1)} %bitcast.76), calls=%async_computation.18 | async-start | bytes 8388608
  235.6 11.6 %slice-start.1 = ((s8[12582912]{0:T(1024)(128)(4,1)}), s8[4194304]{0:T(1024)(128)(4,1)S(1)}, s32[]{:S(2)}) async-start(s8[12582912]{0:T(1024)(128)(4,1)} %bitcast.76), calls=%async_computation.19 | async-start | bytes 8388608
  235.7 13.0 %slice-start.2 = ((s8[12582912]{0:T(1024)(128)(4,1)}), s8[4194304]{0:T(1024)(128)(4,1)S(1)}, s32[]{:S(2)}) async-start(s8[12582912]{0:T(1024)(128)(4,1)} %bitcast.76), calls=%async_computation.20 | async-start | bytes 8388608
  248.7 7.0 copy-start.4
  255.7 2.0 copy-start.2
  257.7 3.2 copy-start.14
  258.8 2.9 copy-start.18
  260.9 0.9 copy-start.12
  274.7 205.1 %reduce-scatter.13.cloned.1.call-start = ((), (), s32[]{:S(2)}) async-start(), calls=%async_computation.12 | async-start | bytes 10616832 | tf_op jit(solution)/shard_map/reduce_scatter | solution.py:280
  282.0 1.4 copy-start.6
  282.1 297.9 %reduce-scatter.15.cloned.1.call-start = ((), (), s32[]{:S(2)}) async-start(), calls=%async_computation.13 | async-start | bytes 10616832 | tf_op jit(solution)/shard_map/reduce_scatter | solution.py:282
  291.7 364.8 %reduce-scatter.21.cloned.1.call-start = ((), (), s32[]{:S(2)}) async-start(), calls=%async_computation.16 | async-start | bytes 442368
  292.8 394.4 %all-reduce.23.cloned.1.call-start = ((), (), s32[]{:S(2)}) async-start(), calls=%async_computation.17 | async-start | bytes 4128768 | tf_op jit(solution)/shard_map/psum | solution.py:291
  301.7 324.5 %copy-start.13 = (bf16[12,64,512]{2,1,0:T(8,128)(2,1)S(1)}, bf16[12,64,512]{2,1,0:T(8,128)(2,1)}, u32[]{:S(2)}) copy-start(bf16[12,64,512]{2,1,0:T(8,128)(2,1)} %copy-done.12) | copy-start | bytes 2359300
  482.0 169.0 %copy-start.10 = (f32[512,768]{1,0:T(8,128)S(1)}, f32[512,768]{1,0:T(8,128)}, u32[]{:S(2)}) copy-start(f32[512,768]{1,0:T(8,128)} %copy-done.9) | copy-start | bytes 4718596
  687.3 7.7 %copy-start.16 = (bf16[384,768]{1,0:T(8,128)(2,1)S(1)}, bf16[384,768]{1,0:T(8,128)(2,1)}, u32[]{:S(2)}) copy-start(bf16[384,768]{1,0:T(8,128)(2,1)} %get-tuple-element.179) | copy-start | bytes 1769476
Sparse Core Ops, SparseCore 0:
  9.6 42.1 all-gather.7
  53.5 22.4 all-gather.9
  77.7 49.5 all-gather.11
  128.8 49.9 all-gather.13
  180.3 22.8 all-gather.15
  228.8 33.0 reduce-scatter.10
  264.2 35.8 reduce-scatter.16
  302.4 77.1 reduce-scatter.18
  381.9 97.8 reduce-scatter.12
  482.0 97.8 reduce-scatter.14
  582.2 28.8 reduce-scatter.20
  615.8 71.4 all-reduce.22
where the time goes:
time: 714 us; the launch traced here: 703 us
  waiting for transfers between devices  373 us (52%)
  blocking collectives  126 us (18%)
  matrix products  103 us (14%)
  other arithmetic  41.2 us (6%)
  local copies, waits for them, and re-layouts  39.3 us (6%)
  between operations  19.6 us (3%)
    reduce_scatter x1, waiting for transfers between devices, body(): lax.psum_scatter(gradients[6], 'fsdp', scatter_dimension=0, tiled=True)  98 us
    reduce_scatter x1, waiting for transfers between devices, body(): lax.psum_scatter(gradients[8], 'fsdp', scatter_dimension=0, tiled=True)  97.9 us
    unnamed x14, waiting for transfers between devices  81.1 us
    unnamed x2, blocking collectives  49.6 us
    psum x1, blocking collectives, body(): bias_total = lax.psum(grad_class_bias, ('dp', 'fsdp'))  42.1 us
    all_gather x1, waiting for transfers between devices, body(): lax.all_gather(down_weight, 'fsdp', axis=0, tiled=True)  31.8 us
    unnamed x85, local copies, waits for them, and re-layouts  31.4 us
    all_gather x1, waiting for transfers between devices, body(): lax.all_gather(up_weight, 'fsdp', axis=0, tiled=True)  27.6 us
  transfers between devices with their start and end apart: 12, of which 8 were waited for; matrix products, arithmetic and copies ran while one was open for 20% of the time, Pallas kernels for 0%

commit v1 on v0

--- a/solution.py
+++ b/solution.py
@@ -1,9 +1,12 @@
+import functools
 from functools import partial
 import math
 
 import jax
 import jax.numpy as jnp
 from jax import lax
+from jax.experimental import pallas as pl
+from jax.experimental.pallas import tpu as pltpu
 from jax.sharding import PartitionSpec as P
 
 H = 12
@@ -33,7 +36,1105 @@
     return jnp.sum(matrix.astype(jnp.float32), axis=0)
 
 
-def body(
+MESH = pl.DeviceIdType.MESH
+
+
+def remote(src, dst, send_sem, recv_sem, target):
+    return pltpu.make_async_remote_copy(
+        src_ref=src, dst_ref=dst, send_sem=send_sem, recv_sem=recv_sem, device_id=target, device_id_type=MESH
+    )
+
+
+class Place:
+    def __init__(self, fsdp_size):
+        self.dp = lax.axis_index("dp")
+        self.shard = lax.axis_index("fsdp")
+        self.line = fsdp_size // 2
+        self.row_half, self.col_half = self.dp // 2, lax.rem(self.dp, 2)
+        self.spot, self.core = self.shard // 2, lax.rem(self.shard, 2)
+        across = 2 * self.row_half + (1 - self.col_half)
+        along = 2 * (1 - self.row_half) + self.col_half
+        self.first = jnp.where(self.core == 0, across, along)
+        self.second = jnp.where(self.core == 0, along, across)
+
+    def partner(self):
+        return {"dp": self.dp, "fsdp": 2 * self.spot + 1 - self.core}
+
+    def on_line(self, hop):
+        return {"dp": self.dp, "fsdp": 2 * lax.rem(self.spot + hop, self.line) + self.core}
+
+    def in_plane(self, dp):
+        return {"dp": dp, "fsdp": self.shard}
+
+    def source_spot(self, hop):
+        return lax.rem(self.spot + self.line - hop, self.line)
+
+    def peers(self):
+        return (
+            [self.partner()]
+            + [self.on_line(hop) for hop in range(1, self.line)]
+            + [self.in_plane(lax.rem(self.dp + step, 4)) for step in range(1, 4)]
+        )
+
+    def meet(self):
+        barrier = pltpu.get_barrier_semaphore()
+        peers = self.peers()
+        for peer in peers:
+            pl.semaphore_signal(barrier, inc=1, device_id=peer, device_id_type=MESH)
+        pl.semaphore_wait(barrier, len(peers))
+
+
+class Gather:
+    def __init__(self, place, shard_ref, whole_ref, send_sems, recv_sems):
+        self.place, self.shard_ref, self.whole = place, shard_ref, whole_ref
+        self.send_sems, self.recv_sems = send_sems, recv_sems
+        self.rows, self.cols = shard_ref.shape
+        self.hops = place.line - 1
+        self.started = []
+
+    @staticmethod
+    def sems(line):
+        return 5 * (line - 1) + 2
+
+    def block(self, shard):
+        return self.whole.at[shard // 2, lax.rem(shard, 2)]
+
+    def quarter(self, shard, row_half, col_half):
+        half_rows, half_cols = self.rows // 2, self.cols // 2
+        return self.whole.at[
+            shard // 2,
+            lax.rem(shard, 2),
+            pl.ds(pl.multiple_of(row_half * half_rows, 16), half_rows),
+            pl.ds(pl.multiple_of(col_half * half_cols, 128), half_cols),
+        ]
+
+    def go(self, index, src, dst, target):
+        copy = remote(src, dst, self.send_sems.at[index], self.recv_sems.at[index], target)
+        copy.start()
+        self.started.append(copy)
+
+    def arrived(self, index, dst):
+        remote(dst, dst, self.send_sems.at[index], self.recv_sems.at[index], self.place.partner()).wait_recv()
+
+    def begin(self):
+        p = self.place
+        half_rows, half_cols = self.rows // 2, self.cols // 2
+        piece = self.shard_ref.at[
+            pl.ds(pl.multiple_of(p.row_half * half_rows, 16), half_rows),
+            pl.ds(pl.multiple_of(p.col_half * half_cols, 128), half_cols),
+        ]
+        for hop in range(1, p.line):
+            self.go(hop - 1, piece, self.quarter(p.shard, p.row_half, p.col_half), p.on_line(hop))
+        self.go(4 * self.hops, self.shard_ref, self.block(p.shard), p.partner())
+        self.own = pltpu.make_async_copy(self.shard_ref, self.block(p.shard), self.recv_sems.at[5 * self.hops + 1])
+        self.own.start()
+
+    def source(self, hop):
+        return 2 * self.place.source_spot(hop) + self.place.core
+
+    def spread(self, hop):
+        p = self.place
+        quarter = self.quarter(self.source(hop), p.row_half, p.col_half)
+        self.arrived(hop - 1, quarter)
+        self.go(self.hops + hop - 1, quarter, quarter, p.in_plane(p.first))
+        self.go(2 * self.hops + hop - 1, quarter, quarter, p.in_plane(p.second))
+
+    def relay(self, hop):
+        p = self.place
+        quarter = self.quarter(self.source(hop), p.first // 2, lax.rem(p.first, 2))
+        self.arrived(self.hops + hop - 1, quarter)
+        self.go(3 * self.hops + hop - 1, quarter, quarter, p.in_plane(p.second))
+
+    def hand(self, hop):
+        p = self.place
+        self.arrived(2 * self.hops + hop - 1, self.quarter(self.source(hop), p.second // 2, lax.rem(p.second, 2)))
+        self.arrived(3 * self.hops + hop - 1, self.quarter(self.source(hop), 1 - p.row_half, 1 - p.col_half))
+        block = self.block(self.source(hop))
+        self.go(4 * self.hops + hop, block, block, p.partner())
+
+    def ready(self):
+        p = self.place
+        self.own.wait()
+        self.arrived(4 * self.hops, self.block(p.shard + 1 - 2 * p.core))
+        for hop in range(1, p.line):
+            self.arrived(4 * self.hops + hop, self.block(2 * p.source_spot(hop) + 1 - p.core))
+
+    def end(self):
+        for copy in self.started:
+            copy.wait_send()
+
+
+class SmallGather:
+    def __init__(self, place, own_ref, all_ref, send_sems, recv_sems):
+        self.place, self.own_ref, self.all = place, own_ref, all_ref
+        self.send_sems, self.recv_sems = send_sems, recv_sems
+        self.hops = place.line - 1
+        self.started = []
+
+    @staticmethod
+    def sems(line):
+        return 2 * (line - 1) + 2
+
+    def go(self, index, src, dst, target):
+        copy = remote(src, dst, self.send_sems.at[index], self.recv_sems.at[index], target)
+        copy.start()
+        self.started.append(copy)
+
+    def arrived(self, index, dst):
+        remote(dst, dst, self.send_sems.at[index], self.recv_sems.at[index], self.place.partner()).wait_recv()
+
+    def begin(self):
+        p = self.place
+        for hop in range(1, p.line):
+            self.go(hop - 1, self.own_ref, self.all.at[p.shard], p.on_line(hop))
+        self.go(2 * self.hops, self.own_ref, self.all.at[p.shard], p.partner())
+        self.own = pltpu.make_async_copy(self.own_ref, self.all.at[p.shard], self.recv_sems.at[2 * self.hops + 1])
+        self.own.start()
+
+    def hand(self):
+        p = self.place
+        for hop in range(1, p.line):
+            block = self.all.at[2 * p.source_spot(hop) + p.core]
+            self.arrived(hop - 1, block)
+            self.go(self.hops + hop - 1, block, block, p.partner())
+
+    def ready(self):
+        p = self.place
+        self.own.wait()
+        self.arrived(2 * self.hops, self.all.at[p.shard + 1 - 2 * p.core])
+        for hop in range(1, p.line):
+            self.arrived(self.hops + hop - 1, self.all.at[2 * p.source_spot(hop) + 1 - p.core])
+
+    def end(self):
+        for copy in self.started:
+            copy.wait_send()
+
+
+class Scatter:
+    def __init__(self, place, grad, from_core, from_first, from_second, from_line, done, send_sems, recv_sems):
+        self.place, self.grad = place, grad
+        self.from_core, self.from_first, self.from_second = from_core, from_first, from_second
+        self.from_line, self.done = from_line, done
+        self.send_sems, self.recv_sems = send_sems, recv_sems
+        self.line, _, self.rows, self.cols = grad.shape
+        self.started = []
+
+    @staticmethod
+    def sems(line):
+        return 1 + 2 + 1 + (line - 1) + 3
+
+    @staticmethod
+    def scratch(line, rows, cols):
+        half = (rows // 2, cols // 2)
+        return [
+            pltpu.VMEM((line, rows, cols), jnp.bfloat16),
+            pltpu.VMEM((2, line) + half, jnp.bfloat16),
+            pltpu.VMEM((line,) + half, jnp.bfloat16),
+            pltpu.VMEM((line - 1,) + half, jnp.bfloat16),
+            pltpu.VMEM((2, 2) + half, jnp.bfloat16),
+        ]
+
+    def go(self, index, src, dst, target):
+        copy = remote(src, dst, self.send_sems.at[index], self.recv_sems.at[index], target)
+        copy.start()
+        self.started.append(copy)
+
+    def arrived(self, index, dst):
+        remote(dst, dst, self.send_sems.at[index], self.recv_sems.at[index], self.place.partner()).wait_recv()
+
+    def slices(self, row_half, col_half):
+        half_rows, half_cols = self.rows // 2, self.cols // 2
+        return (
+            pl.ds(pl.multiple_of(row_half * half_rows, 16), half_rows),
+            pl.ds(pl.multiple_of(col_half * half_cols, 128), half_cols),
+        )
+
+    def halves(self, side, which):
+        p = self.place
+        row_half = jnp.where(p.core == 0, which, side)
+        col_half = jnp.where(p.core == 0, side, which)
+        return self.slices(row_half, col_half)
+
+    def swap(self):
+        p = self.place
+        self.go(0, self.grad.at[:, 1 - p.core], self.from_core, p.partner())
+
+    def add(self, rows, cols, others, targets_spot=None):
+        p = self.place
+        half_rows, half_cols = self.rows // 2, self.cols // 2
+        step = 48 if half_rows % 48 == 0 else 16
+        steps = half_rows // step
+
+        def one(index, carry):
+            spot, part = index // steps, lax.rem(index, steps)
+            at = pl.ds(pl.multiple_of(rows.start + part * step, 16), step)
+            inner = pl.ds(pl.multiple_of(part * step, 16), step)
+            total = self.grad[spot, p.core, at, cols].astype(jnp.float32) + self.from_core[spot, at, cols].astype(
+                jnp.float32
+            )
+            for other in others:
+                total = total + other[spot, inner, :].astype(jnp.float32)
+            self.grad[spot, p.core, at, cols] = total.astype(jnp.bfloat16)
+            return carry
+
+        lax.fori_loop(0, self.line * steps, one, 0)
+
+    def to_first(self):
+        p = self.place
+        self.arrived(0, self.from_core)
+        keep = jnp.where(p.core == 0, p.col_half, p.row_half)
+        for which in (0, 1):
+            rows, cols = self.halves(1 - keep, which)
+            self.add(rows, cols, [])
+            self.go(1 + which, self.grad.at[:, p.core, rows, cols], self.from_first.at[which], p.in_plane(p.first))
+
+    def to_second(self):
+        p = self.place
+        for which in (0, 1):
+            self.arrived(1 + which, self.from_first.at[which])
+        keep = jnp.where(p.core == 0, p.col_half, p.row_half)
+        mine = jnp.where(p.core == 0, p.row_half, p.col_half)
+        rows, cols = self.halves(keep, 1 - mine)
+        self.add(rows, cols, [self.from_first.at[1 - mine]])
+        self.go(3, self.grad.at[:, p.core, rows, cols], self.from_second, p.in_plane(p.second))
+
+    def to_line(self):
+        p = self.place
+        self.arrived(3, self.from_second)
+        mine = jnp.where(p.core == 0, p.row_half, p.col_half)
+        rows, cols = self.slices(p.row_half, p.col_half)
+        self.add(rows, cols, [self.from_first.at[mine], self.from_second])
+        for hop in range(1, self.line):
+            spot = lax.rem(p.spot + hop, self.line)
+            self.go(3 + hop, self.grad.at[spot, p.core, rows, cols], self.from_line.at[hop - 1], p.on_line(hop))
+
+    def to_plane(self):
+        p = self.place
+        for hop in range(1, self.line):
+            self.arrived(3 + hop, self.from_line.at[hop - 1])
+        half_rows = self.rows // 2
+        rows, cols = self.slices(p.row_half, p.col_half)
+        step = 16
+
+        def one(part, carry):
+            at = pl.ds(pl.multiple_of(rows.start + part * step, 16), step)
+            inner = pl.ds(pl.multiple_of(part * step, 16), step)
+            total = self.grad[p.spot, p.core, at, cols].astype(jnp.float32)
+            for hop in range(1, self.line):
+                total = total + self.from_line[hop - 1, inner, :].astype(jnp.float32)
+            self.done[p.row_half, p.col_half, inner, :] = total.astype(jnp.bfloat16)
+            return carry
+
+        lax.fori_loop(0, half_rows // step, one, 0)
+        own = self.done.at[p.row_half, p.col_half]
+        for step in range(1, 4):
+            self.go(2 + self.line + step, own, own, p.in_plane(lax.rem(p.dp + step, 4)))
+
+    def finish(self):
+        p = self.place
+        for step in range(1, 4):
+            other = lax.rem(p.dp + 4 - step, 4)
+            self.arrived(2 + self.line + step, self.done.at[other // 2, lax.rem(other, 2)])
+
+    def end(self):
+        for copy in self.started:
+            copy.wait_send()
+
+
+class SmallSum:
+    def __init__(self, place, own, from_core, on_line, in_plane, send_sems, recv_sems):
+        self.place, self.own, self.from_core, self.on_line, self.in_plane = place, own, from_core, on_line, in_plane
+        self.send_sems, self.recv_sems = send_sems, recv_sems
+        self.started = []
+
+    @staticmethod
+    def sems(line):
+        return 1 + (line - 1) + 3
+
+    @staticmethod
+    def scratch(line, rows, cols):
+        return [
+            pltpu.VMEM((rows, cols), jnp.float32),
+            pltpu.VMEM((rows, cols), jnp.float32),
+            pltpu.VMEM((line, rows, cols), jnp.float32),
+            pltpu.VMEM((4, rows, cols), jnp.float32),
+        ]
+
+    def go(self, index, src, dst, target):
+        copy = remote(src, dst, self.send_sems.at[index], self.recv_sems.at[index], target)
+        copy.start()
+        self.started.append(copy)
+
+    def arrived(self, index, dst):
+        remote(dst, dst, self.send_sems.at[index], self.recv_sems.at[index], self.place.partner()).wait_recv()
+
+    def swap(self):
+        self.go(0, self.own, self.from_core, self.place.partner())
+
+    def to_line(self):
+        p = self.place
+        self.arrived(0, self.from_core)
+        self.on_line[p.spot] = self.own[...] + self.from_core[...]
+        slot = self.on_line.at[p.spot]
+        for hop in range(1, p.line):
+            self.go(hop, slot, slot, p.on_line(hop))
+
+    def to_plane(self):
+        p = self.place
+        for hop in range(1, p.line):
+            self.arrived(hop, self.on_line.at[p.source_spot(hop)])
+        total = self.on_line[0]
+        for spot in range(1, p.line):
+            total = total + self.on_line[spot]
+        self.in_plane[p.dp] = total
+        slot = self.in_plane.at[p.dp]
+        for step in range(1, 4):
+            self.go(p.line - 1 + step, slot, slot, p.in_plane(lax.rem(p.dp + step, 4)))
+
+    def finish(self, out_ref):
+        p = self.place
+        for step in range(1, 4):
+            self.arrived(p.line - 1 + step, self.in_plane.at[lax.rem(p.dp + 4 - step, 4)])
+        out_ref[...] = (self.in_plane[0] + self.in_plane[1]) + (self.in_plane[2] + self.in_plane[3])
+
+    def end(self):
+        for copy in self.started:
+            copy.wait_send()
+
+
+class SequenceGather:
+    def __init__(self, place, blocks, send_sems, recv_sems):
+        self.place, self.blocks = place, blocks
+        self.send_sems, self.recv_sems = send_sems, recv_sems
+        self.started = []
+
+    @staticmethod
+    def sems(line):
+        return 3 + (line - 1) + line
+
+    def go(self, index, ref, target):
+        copy = remote(ref, ref, self.send_sems.at[index], self.recv_sems.at[index], target)
+        copy.start()
+        self.started.append(copy)
+
+    def arrived(self, index, dst):
+        remote(dst, dst, self.send_sems.at[index], self.recv_sems.at[index], self.place.partner()).wait_recv()
+
+    def begin(self):
+        p = self.place
+        for step in range(1, 4):
+            self.go(step - 1, self.blocks.at[p.shard, p.dp], p.in_plane(lax.rem(p.dp + step, 4)))
+
+    def to_line(self):
+        p = self.place
+        for step in range(1, 4):
+            self.arrived(step - 1, self.blocks.at[p.shard, lax.rem(p.dp + 4 - step, 4)])
+        own = self.blocks.at[p.shard]
+        for hop in range(1, p.line):
+            self.go(2 + hop, own, p.on_line(hop))
+        self.go(2 + p.line, own, p.partner())
+
+    def hand(self):
+        p = self.place
+        for hop in range(1, p.line):
+            block = self.blocks.at[2 * p.source_spot(hop) + p.core]
+            self.arrived(2 + hop, block)
+            self.go(2 + p.line + hop, block, p.partner())
+
+    def ready(self):
+        p = self.place
+        self.arrived(2 + p.line, self.blocks.at[p.shard + 1 - 2 * p.core])
+        for hop in range(1, p.line):
+            self.arrived(2 + p.line + hop, self.blocks.at[2 * p.source_spot(hop) + 1 - p.core])
+
+    def end(self):
+        for copy in self.started:
+            copy.wait_send()
+ANY = pl.BlockSpec(memory_space=pl.ANY)
+WHOLE = pl.BlockSpec(memory_space=pltpu.VMEM)
+SCALARS = pl.BlockSpec(memory_space=pltpu.SMEM)
+VMEM_BYTES = 67_000_000
+BF16, F32 = jnp.bfloat16, jnp.float32
+
+
+def nn(left, right):
+    return lax.dot_general(left, right, (((1,), (0,)), ((), ())), preferred_element_type=F32)
+
+
+def nt(left, right):
+    return lax.dot_general(left, right, (((1,), (1,)), ((), ())), preferred_element_type=F32)
+
+
+def tn(left, right):
+    return lax.dot_general(left, right, (((0,), (0,)), ((), ())), preferred_element_type=F32)
+
+
+def lanes(start, size):
+    return pl.ds(pl.multiple_of(start, 128), size)
+
+
+def loop(count, step):
+    def one(index, carry):
+        step(index)
+        return carry
+
+    lax.fori_loop(0, count, one, 0)
+
+
+def gelu_parts(v):
+    spread = 0.5 * (1.0 + lax.erf(v * (1.0 / math.sqrt(2.0))))
+    bell = jnp.exp(-0.5 * v * v) * (1.0 / math.sqrt(2.0 * math.pi))
+    return v * spread, spread + v * bell
+
+
+def place_vectors(shard, vectors, class_rows, short, out):
+    in_bias, mix_bias, gain_one, shift_one, up_bias, down_bias, gain_two, shift_two, pool_bias = vectors
+    short[...] = jnp.zeros(short.shape, F32)
+    rows = [in_bias, in_bias, mix_bias, gain_one, shift_one, up_bias, up_bias, up_bias, up_bias]
+    rows += [down_bias, gain_two, shift_two, pool_bias]
+    for row, vector in enumerate(rows):
+        size = vector.shape[0]
+        short[row : row + 1, 0:size] = vector[...].astype(F32).reshape(1, size)
+    size = class_rows.shape[1]
+    short[13 : 13 + class_rows.shape[0], 0:size] = class_rows[...].astype(F32)
+    values = short[...].astype(BF16)
+    span, width = short.shape[1], out.shape[1]
+    lane = lax.broadcasted_iota(jnp.int32, (span, width), 0)
+    column = lax.broadcasted_iota(jnp.int32, (span, width), 1)
+    row_at = lax.broadcasted_iota(jnp.int32, (16, 1), 0)
+
+    def placed(size):
+        per_row = width // size
+        spread = jnp.where((column - lax.rem(shard, per_row) * size == lane) & (lane < size), 1.0, 0.0)
+        return nn(values, spread.astype(BF16)), shard // per_row
+
+    one_row, _ = placed(mix_bias.shape[0])
+    of_in, in_row = placed(in_bias.shape[0])
+    of_up, up_row = placed(up_bias.shape[0])
+    is_in, is_up = row_at < 2, (row_at >= 5) & (row_at < 9)
+    result = jnp.where(is_in, jnp.where(row_at == in_row, of_in, 0.0), one_row)
+    result = jnp.where(is_up, jnp.where(row_at == 5 + up_row, of_up, 0.0), result)
+    out[...] = result.astype(BF16)
+
+
+def own_sums(shard, parts, total_ref, out, classes):
+    total = total_ref[...]
+    width = total.shape[1]
+    size = width // parts
+    own, own_in, own_up = (jnp.zeros(shape, F32) for shape in ((24, size), (1, 2 * size), (1, 4 * size)))
+    for place in range(parts):
+        here = shard == place
+        own = jnp.where(here, total[:, place * size : (place + 1) * size], own)
+        row, at = divmod(2 * size * place, width)
+        own_in = jnp.where(here, total[row : row + 1, at : at + 2 * size], own_in)
+        row, at = divmod(4 * size * place, width)
+        own_up = jnp.where(here, total[5 + row : 6 + row, at : at + 4 * size], own_up)
+    out[...] = jnp.zeros(out.shape, F32)
+    out[0:24, 0:size] = own
+    out[24:25, 0 : 2 * size] = own_in
+    out[25:26, 0 : 4 * size] = own_up
+    out[26:27, 0:classes] = total[16:17, 13 : 13 + classes]
+
+
+def layer_kernel(fsdp_size, *refs):
+    refs = list(refs)
+
+    def take(count):
+        out = refs[:count]
+        del refs[:count]
+        return out
+
+    lengths, labels, class_bias, tokens_in, cot_in = take(5)
+    shards = take(5)
+    vectors, class_rows = take(9), take(1)[0]
+    layer_out, input_grad, down_out, up_out, mix_out, in_out, pool_out, sums_out = take(8)
+    w_in, w_mix, w_up, w_down, w_pool, small_all = take(6)
+    g_down, g_up = take(2)
+    recv = [take(5) for _ in range(4)]
+    sum_refs = take(4)
+    (blocks,) = take(1)
+    tok, tok_t, cot, att, att_t, first, first_t = take(7)
+    qkv, act, slope = take(3)
+    unit_one, unit_two, grad = take(3)
+    inv_one, inv_two, key_mask, lse, vec = take(5)
+    short, small_in, bias_row, sums_all = take(4)
+    g_send, g_recv, s_send, s_recv, q_send, q_recv, v_send, v_recv, b_send, b_recv, local = take(11)
+    seq, width = tok.shape
+    hidden = act.shape[1]
+    pairs = width // 128
+    parts = hidden // width
+    line = fsdp_size // 2
+    rows_of = pl.ds
+
+    loads = [
+        pltpu.make_async_copy(tokens_in, tok, local.at[0]),
+        pltpu.make_async_copy(cot_in, cot, local.at[1]),
+    ]
+    for load in loads:
+        load.start()
+    place = Place(fsdp_size)
+    place_vectors(place.shard, vectors, class_rows, short, small_in)
+    bias_row[...] = jnp.zeros(bias_row.shape, F32)
+    classes = class_bias.shape[0]
+    bias_row[0:1, 13 : 13 + classes] = class_bias[...].astype(F32).reshape(1, classes)
+    place.meet()
+    gathers = [
+        Gather(place, shard, whole, g_send.at[i], g_recv.at[i])
+        for i, (shard, whole) in enumerate(zip(shards, (w_in, w_mix, w_up, w_down, w_pool)))
+    ]
+    for_in, for_mix, for_up, for_down, for_pool = gathers
+    little = SmallGather(place, small_in, small_all, v_send, v_recv)
+    for_in.begin()
+    little.begin()
+    for one in gathers[1:]:
+        one.begin()
+    hops = range(1, line)
+    length = lengths[0]
+    label = labels[0]
+
+    for load in loads:
+        load.wait()
+    tok_t[...] = tok[...].T
+    key_at = lax.broadcasted_iota(jnp.int32, (seq, 128), 0)
+    key_mask[...] = jnp.where(key_at < length, 0.0, -1e30).astype(F32)
+
+    def mask_cot(index):
+        rows = rows_of(pl.multiple_of(index * 128, 128), 128)
+        live = (key_mask[rows, :] == 0.0).astype(F32)
+        grad[rows, :] = cot[rows, :].astype(F32) * jnp.concatenate([live] * (width // 128), axis=1)
+
+    loop(seq // 128, mask_cot)
+    grad_low = cot
+
+    for hop in hops:
+        for_in.spread(hop)
+    little.hand()
+    for hop in hops:
+        for_in.relay(hop)
+    for hop in hops:
+        for_mix.spread(hop)
+    little.ready()
+    vec[...] = jnp.sum(small_all[...].astype(F32), axis=0)
+    for hop in hops:
+        for_in.hand(hop)
+    for hop in hops:
+        for_mix.relay(hop)
+    for_in.ready()
+
+    score_scale = 1.0 / math.sqrt(DH)
+    for part in range(3):
+
+        def project(index, part=part):
+            inner = lanes(index * 256, 256)
+            cols = lanes(part * width + index * 256, 256)
+            out = nn(tok[...], w_in[:, :, :, cols].reshape(width, 256))
+            if part != 1:
+                row = 0 if part == 0 else 1
+                out = out + vec[row : row + 1, inner]
+            out = out.astype(BF16)
+            if part == 0:
+                out = out * jnp.asarray(score_scale, BF16)
+            qkv[:, cols] = out
+
+        loop(width // 256, project)
+    for hop in hops:
+        for_mix.hand(hop)
+
+    low_lanes = lax.broadcasted_iota(jnp.int32, (1, 128), 1) < 64
+    zero_low = jnp.zeros((), BF16)
+
+    def head_lanes(value, half):
+        return jnp.where(low_lanes if half == 0 else jnp.logical_not(low_lanes), value, zero_low)
+
+    def masked_scores(keys, queries):
+        mask = key_mask[...]
+        return nt(keys, queries) + jnp.concatenate([mask] * (seq // 128), axis=1)
+
+    def attend(pair):
+        queries, keys, values = (qkv[:, lanes(part * width + pair * 128, 128)] for part in range(3))
+        values_t = values.T
+        mixed = []
+        for half in (0, 1):
+            scores = masked_scores(keys, head_lanes(queries, half))
+            highest = jnp.max(scores, axis=0, keepdims=True)
+            raw = jnp.exp(scores - highest)
+            total = jnp.sum(raw, axis=0, keepdims=True)
+            lse[pair, half : half + 1, :] = highest + jnp.log(total)
+            soft = (raw * (1.0 / total)).astype(BF16)
+            mixed.append(nn(values_t, soft)[64 * half : 64 * half + 64, :])
+        both = jnp.concatenate(mixed, axis=0)
+        att_t[rows_of(pl.multiple_of(pair * 128, 128), 128), :] = both.astype(BF16)
+        att[:, lanes(pair * 128, 128)] = both.T.astype(BF16)
+
+    def attend_some(first_pair, last_pair):
+        lax.fori_loop(first_pair, last_pair, lambda pair, carry: (attend(pair), carry)[1], 0)
+
+    attend_some(0, 2)
+    for hop in hops:
+        for_up.spread(hop)
+    attend_some(2, 4)
+    for hop in hops:
+        for_up.relay(hop)
+    attend_some(4, pairs)
+    for hop in hops:
+        for_down.spread(hop)
+    for hop in hops:
+        for_up.hand(hop)
+    for_mix.ready()
+
+    gain_one, shift_one = vec[3:4, :], vec[4:5, :]
+
+    def mean_of(value):
+        return jnp.sum(value, axis=1, keepdims=True) * (1.0 / width)
+
+    def norm_one(index):
+        rows = rows_of(pl.multiple_of(index * 256, 256), 256)
+        total = nn(att[rows, :], w_mix[...].reshape(width, width)) + vec[2:3, :] + tok[rows, :].astype(F32)
+        centered = total - mean_of(total)
+        inverse = lax.rsqrt(mean_of(centered * centered) + EPSILON)
+        unit = centered * inverse
+        unit_one[rows, :] = unit
+        inv_one[rows, :] = jnp.broadcast_to(inverse, (256, 128))
+        first[rows, :] = (unit * gain_one + shift_one).astype(BF16)
+
+    loop(seq // 256, norm_one)
+    first_t[...] = first[...].T
+    for hop in hops:
+        for_down.relay(hop)
+    for hop in hops:
+        for_pool.spread(hop)
+    for_up.ready()
+
+    for part in range(parts):
+
+        def raise_up(index, part=part):
+            inner = lanes(index * 384, 384)
+            cols = lanes(part * width + index * 384, 384)
+            pre = nn(first[...], w_up[:, :, :, cols].reshape(width, 384)) + vec[5 + part : 6 + part, inner]
+            value, derivative = gelu_parts(pre)
+            act[:, cols] = value.astype(BF16)
+            slope[:, cols] = derivative.astype(BF16)
+
+        loop(width // 384, raise_up)
+        if part == 0:
+            for hop in hops:
+                for_down.hand(hop)
+        if part == 1:
+            for hop in hops:
+                for_pool.relay(hop)
+    for hop in hops:
+        for_pool.hand(hop)
+    for_down.ready()
+    gain_two, shift_two = vec[10:11, :], vec[11:12, :]
+
+    def norm_two(index):
+        rows = rows_of(pl.multiple_of(index * 256, 256), 256)
+        total = nn(act[rows, :], w_down[...].reshape(hidden, width)) + vec[9:10, :]
+        total = total + (unit_one[rows, :] * gain_one + shift_one)
+        centered = total - mean_of(total)
+        inverse = lax.rsqrt(mean_of(centered * centered) + EPSILON)
+        unit = centered * inverse
+        unit_two[rows, :] = unit
+        inv_two[rows, :] = jnp.broadcast_to(inverse, (256, 128))
+        att[rows, :] = (unit * gain_two + shift_two).astype(BF16)
+
+    loop(seq // 256, norm_two)
+    stores = [pltpu.make_async_copy(att, layer_out, local.at[2])]
+    stores[0].start()
+
+    for_pool.ready()
+    top = lax.broadcasted_iota(jnp.int32, (16, 1), 0) == 0
+    head = att[0:16, :]
+    vec_low = vec[...].astype(BF16)
+    pooled = jnp.tanh(nn(head, w_pool[...].reshape(width, width)) + vec[12:13, :])
+    pooled_low = pooled.astype(BF16)
+    logits = nt(pooled_low, vec_low) + bias_row[0:1, 0:16]
+    class_at = lax.broadcasted_iota(jnp.int32, (16, 16), 1) - 13
+    logits = jnp.where(class_at >= 0, logits, -1e30)
+    raised = jnp.exp(logits - jnp.max(logits, axis=1, keepdims=True))
+    soft_logits = raised / jnp.sum(raised, axis=1, keepdims=True)
+    onehot = (class_at == label).astype(F32)
+    grad_logits = jnp.where(top, soft_logits - onehot, 0.0).astype(BF16)
+    sums = sum_refs[0]
+    sums[0:16, :] = tn(grad_logits, pooled_low)
+    sums[16:24, :] = jnp.zeros((8, width), F32)
+    sums[16:17, 0:16] = grad_logits[0:1, :].astype(F32)
+    grad_pool_pre = (nn(grad_logits, vec_low) * (1.0 - pooled * pooled)).astype(BF16)
+    sums[12:13, :] = grad_pool_pre[0:1, :].astype(F32)
+    block = jnp.where(top, head.astype(F32), 0.0)
+    second_row = lax.broadcasted_iota(jnp.int32, (16, 1), 0) == 1
+    block = jnp.where(second_row, jnp.broadcast_to(grad_pool_pre[0:1, :].astype(F32), (16, width)), block)
+    blocks[place.shard, place.dp] = block.astype(BF16)
+    sequences = SequenceGather(place, blocks, q_send, q_recv)
+    sequences.begin()
+    grad[0:16, :] += nt(grad_pool_pre, w_pool[...].reshape(width, width))
+
+    for one in gathers:
+        one.end()
+
+    def norm_back(unit_ref, inv_ref, gain, gain_row, shift_row, bias_row, size):
+        def one(index, carry):
+            by_gain, by_shift, by_bias = carry
+            rows = rows_of(pl.multiple_of(index * size, size), size)
+            incoming = grad[rows, :]
+            unit = unit_ref[rows, :]
+            scaled = incoming * gain
+            inverse = jnp.concatenate([inv_ref[rows, :]] * (width // 128), axis=1)
+            back = inverse * (scaled - mean_of(scaled) - unit * mean_of(scaled * unit))
+            low = back.astype(BF16)
+            grad[rows, :] = back
+            grad_low[rows, :] = low
+            return (
+                by_gain + jnp.sum(incoming * unit, axis=0, keepdims=True),
+                by_shift + jnp.sum(incoming, axis=0, keepdims=True),
+                by_bias + jnp.sum(low.astype(F32), axis=0, keepdims=True),
+            )
+
+        zero = jnp.zeros((1, width), F32)
+        by_gain, by_shift, by_bias = lax.fori_loop(0, seq // size, one, (zero, zero, zero))
+        sums[gain_row : gain_row + 1, :] = by_gain
+        sums[shift_row : shift_row + 1, :] = by_shift
+        sums[bias_row : bias_row + 1, :] = by_bias
+
+    norm_back(unit_two, inv_two, gain_two, 10, 11, 9, 128)
+
+    scatters = [
+        Scatter(place, ref, *recv[i], s_send.at[i], s_recv.at[i])
+        for i, ref in enumerate((g_down, g_up, w_up.at[:, :, :, pl.ds(3 * width, width)], w_up.at[:, :, :, pl.ds(0, 3 * width)]))
+    ]
+    of_down, of_up, of_mix, of_in = scatters
+    rows_down = hidden // fsdp_size
+
+    def down_gradient(index):
+        cols = lanes(index * rows_down, rows_down)
+        g_down[index // 2, lax.rem(index, 2)] = tn(act[:, cols], grad_low[...]).astype(BF16)
+
+    loop(fsdp_size, down_gradient)
+    of_down.swap()
+    sequences.to_line()
+
+    for part in range(parts):
+
+        def through_down(index, part=part):
+            owner = part * 2 + index
+            inner = lanes(index * rows_down, rows_down)
+            cols = lanes(owner * rows_down, rows_down)
+            low = (nt(grad_low[...], w_down[part, index]) * slope[:, cols].astype(F32)).astype(BF16)
+            slope[:, cols] = low
+            sums[5 + part : 6 + part, inner] = jnp.sum(low.astype(F32), axis=0, keepdims=True)
+
+        loop(2, through_down)
+        if part == 1:
+            of_down.to_first()
+
+    def up_gradient(index):
+        cols = lanes(index * 256, 256)
+        out = nn(first_t[...], slope[:, cols]).astype(BF16)
+        g_up[:, :, :, cols] = out.reshape(line, 2, width // fsdp_size, 256)
+
+    loop(hidden // 256, up_gradient)
+    of_up.swap()
+    of_down.to_second()
+    sequences.hand()
+
+    half_line = line // 2
+    half_width = width // 2
+
+    def through_up(index):
+        cols = lanes(index * half_width, half_width)
+        weight = w_up[rows_of(index * half_line, half_line)].reshape(half_width, hidden)
+        grad[:, cols] += nt(slope[...], weight)
+
+    loop(2, through_up)
+    of_up.to_first()
+    of_down.to_line()
+    norm_back(unit_one, inv_one, gain_one, 3, 4, 2, 128)
+
+    def mix_gradient(index):
+        out = nn(att_t[...], grad_low[:, lanes(index * 256, 256)]).astype(BF16)
+        w_up[:, :, :, lanes(3 * width + index * 256, 256)] = out.reshape(line, 2, width // fsdp_size, 256)
+
+    loop(width // 256, mix_gradient)
+    of_mix.swap()
+
+    def through_mix(index):
+        cols = lanes(index * half_width, half_width)
+        weight = w_mix[rows_of(index * half_line, half_line)].reshape(half_width, width)
+        first[:, cols] = nt(grad_low[...], weight).astype(BF16)
+
+    loop(2, through_mix)
+    of_up.to_second()
+
+    def attend_back(pair):
+        at = [lanes(part * width + pair * 128, 128) for part in range(3)]
+        queries, keys, values = (qkv[:, cols] for cols in at)
+        rows = rows_of(pl.multiple_of(pair * 128, 128), 128)
+        out_grad = first[:, lanes(pair * 128, 128)]
+        keys_t = keys.T
+        products = out_grad.astype(F32).T * att_t[rows, :].astype(F32)
+        by_query, by_key, by_value = [], None, None
+        for half in (0, 1):
+            own_queries, own_grad = head_lanes(queries, half), head_lanes(out_grad, half)
+            soft = jnp.exp(masked_scores(keys, own_queries) - lse[pair, half : half + 1, :])
+            row_sum = jnp.sum(products[64 * half : 64 * half + 64, :], axis=0, keepdims=True)
+            score_grad = (soft * (nt(values, own_grad) - row_sum)).astype(BF16)
+            value_part = nn(soft.astype(BF16), own_grad)
+            key_part = nn(score_grad, own_queries)
+            by_value = value_part if by_value is None else by_value + value_part
+            by_key = key_part if by_key is None else by_key + key_part
+            by_query.append(nn(keys_t, score_grad)[64 * half : 64 * half + 64, :])
+        qkv[:, at[0]] = (jnp.concatenate(by_query, axis=0).T * score_scale).astype(BF16)
+        qkv[:, at[1]] = by_key.astype(BF16)
+        qkv[:, at[2]] = by_value.astype(BF16)
+
+    def attend_back_some(first_pair, last_pair):
+        lax.fori_loop(first_pair, last_pair, lambda pair, carry: (attend_back(pair), carry)[1], 0)
+
+    attend_back_some(0, 1)
+    of_mix.to_first()
+    of_down.to_plane()
+    attend_back_some(1, 2)
+    of_up.to_line()
+    attend_back_some(2, 3)
+    of_mix.to_second()
+    attend_back_some(3, 4)
+    sequences.ready()
+    attend_back_some(4, 5)
+    of_up.to_plane()
+    of_mix.to_line()
+    attend_back_some(5, pairs)
+
+    for part in range(3):
+
+        def in_gradient(index, part=part):
+            inner = lanes(index * 256, 256)
+            cols = lanes(part * width + index * 256, 256)
+            incoming = qkv[:, cols]
+            w_up[:, :, :, cols] = nn(tok_t[...], incoming).astype(BF16).reshape(line, 2, width // fsdp_size, 256)
+            if part != 1:
+                row = 0 if part == 0 else 1
+                sums[row : row + 1, inner] = jnp.sum(incoming.astype(F32), axis=0, keepdims=True)
+
+        loop(width // 256, in_gradient)
+    of_in.swap()
+    total = SmallSum(place, *sum_refs, b_send, b_recv)
+    total.swap()
+    of_mix.to_plane()
+
+    def through_in(index):
+        cols = lanes(index * half_width, half_width)
+        weight = w_in[rows_of(index * half_line, half_line)].reshape(half_width, 3 * width)
+        grad[:, cols] += nt(qkv[...], weight)
+
+    loop(1, through_in)
+    of_in.to_first()
+    total.to_line()
+    loop_from_one = lambda step: lax.fori_loop(1, 2, lambda index, carry: (step(index), carry)[1], 0)
+    loop_from_one(through_in)
+    store = pltpu.make_async_copy(grad, input_grad, local.at[3])
+    store.start()
+    stores.append(store)
+    of_in.to_second()
+    total.to_plane()
+
+    every = blocks[...].reshape(fsdp_size * 4 * 16, width)
+    count = fsdp_size * 4 * 16
+    row_at = lax.broadcasted_iota(jnp.int32, (count, count), 0)
+    col_at = lax.broadcasted_iota(jnp.int32, (count, count), 1)
+    shift = jnp.where((lax.rem(row_at, 16) == 0) & (col_at == row_at + 1), 1.0, 0.0).astype(BF16)
+    paired = nn(shift, every).astype(BF16)
+    own_rows_at = lax.broadcasted_iota(jnp.int32, (128, width), 0) + place.shard * (width // fsdp_size)
+    pick = jnp.where(own_rows_at == lax.broadcasted_iota(jnp.int32, (128, width), 1), 1.0, 0.0).astype(BF16)
+    own_part = nt(pick, every).astype(BF16)
+    pool_out[...] = nn(own_part, paired)[0 : width // fsdp_size, :]
+
+    of_in.to_line()
+    total.finish(sums_all)
+    own_sums(place.shard, fsdp_size, sums_all, sums_out, classes)
+    of_in.to_plane()
+    for index, (one, out) in enumerate(zip(scatters, (down_out, up_out, mix_out, in_out))):
+        one.finish()
+        half_rows, half_cols = one.rows // 2, one.cols // 2
+        for quarter in range(4):
+            row_half, col_half = quarter // 2, quarter % 2
+            target = out.at[
+                pl.ds(row_half * half_rows, half_rows), pl.ds(col_half * half_cols, half_cols)
+            ]
+            store = pltpu.make_async_copy(one.done.at[row_half, col_half], target, local.at[4 + 4 * index + quarter])
+            store.start()
+            stores.append(store)
+    for store in stores:
+        store.wait()
+    for one in scatters + [little, sequences, total]:
+        one.end()
+
+
+def run_layer(fsdp_size, lengths, labels, class_bias, tokens, cotangent, shards, vectors, class_rows):
+    line = fsdp_size // 2
+    seq, width = tokens.shape
+    in_shard, mix_shard, up_shard, down_shard, pool_shard = shards
+    hidden = up_shard.shape[1]
+    vmem, dma = pltpu.VMEM, pltpu.SemaphoreType.DMA
+    reduced = (down_shard, up_shard, mix_shard, in_shard)
+    scratch = [vmem((line, 2) + s.shape, BF16) for s in shards] + [vmem((fsdp_size, 16, width), BF16)]
+    scratch += [vmem((line, 2) + s.shape, BF16) for s in (down_shard, up_shard)]
+    for s in reduced:
+        scratch += Scatter.scratch(line, *s.shape)
+    scratch += SmallSum.scratch(line, 24, width)
+    scratch += [vmem((fsdp_size, 4, 16, width), BF16)]
+    rows, turned = vmem((seq, width), BF16), vmem((width, seq), BF16)
+    scratch += [rows, turned, rows, rows, turned, rows, turned]
+    scratch += [vmem((seq, 3 * width), BF16), vmem((seq, hidden), BF16), vmem((seq, hidden), BF16)]
+    scratch += [vmem((seq, width), F32)] * 3
+    scratch += [vmem((seq, 128), F32)] * 3 + [vmem((width // 128, 8, seq), F32), vmem((16, width), F32)]
+    span = hidden // fsdp_size
+    scratch += [vmem((16, span), F32), vmem((16, width), BF16), vmem((8, 128), F32), vmem((24, width), F32)]
+    for count in (
+        (5, Gather.sems(line)),
+        (4, Scatter.sems(line)),
+        (SequenceGather.sems(line),),
+        (SmallGather.sems(line),),
+        (SmallSum.sems(line),),
+    ):
+        scratch += [dma(count), dma(count)]
+    scratch += [dma((20,))]
+    out_shape = [jax.ShapeDtypeStruct((seq, width), BF16), jax.ShapeDtypeStruct((seq, width), F32)]
+    out_shape += [jax.ShapeDtypeStruct(s.shape, BF16) for s in reduced]
+    out_shape += [jax.ShapeDtypeStruct((width // fsdp_size, width), F32), jax.ShapeDtypeStruct((32, span), F32)]
+    return pl.pallas_call(
+        functools.partial(layer_kernel, fsdp_size),
+        out_shape=out_shape,
+        in_specs=[SCALARS, SCALARS, WHOLE] + [ANY] * 7 + [WHOLE] * 10,
+        out_specs=[ANY] * 6 + [WHOLE] * 2,
+        scratch_shapes=scratch,
+        compiler_params=pltpu.CompilerParams(collective_id=0, has_side_effects=True, vmem_limit_bytes=VMEM_BYTES),
+        name="layer",
+    )(lengths, labels, class_bias, tokens, cotangent, *shards, *vectors, class_rows)
+
+
+def outputs_kernel(as_is, rounded, sizes, classes, size, *refs):
+    count = as_is + rounded
+    inputs, sums = refs[:count], refs[count]
+    refs = refs[count + 1 :]
+    outs, small = refs[:count], refs[count : count + len(sizes) + 2]
+    refs = refs[count + len(sizes) + 2 :]
+    held, wide, (load_sems, store_sems) = refs[:count], refs[count : count + rounded], refs[count + rounded :]
+    order = list(range(as_is, count)) + list(range(as_is))
+    loads = {i: pltpu.make_async_copy(inputs[i], held[i], load_sems.at[i]) for i in order}
+    for load in loads.values():
+        load.start()
+    for (row, length), out in zip(sizes.items(), small):
+        out[...] = sums[row : row + 1, 0:length].reshape(length)
+    small[-2][...] = sums[13 : 13 + classes, 0:size]
+    small[-1][...] = sums[26:27, 0:classes].reshape(classes)
+    stores = []
+    for i in order:
+        loads[i].wait()
+        source = held[i]
+        if i >= as_is:
+            source = wide[i - as_is]
+            step = 32
+
+            def widen(index, narrow=held[i], source=source):
+                rows = pl.ds(pl.multiple_of(index * step, step), step)
+                source[rows, :] = narrow[rows, :].astype(F32)
+
+            loop(source.shape[0] // step, widen)
+        stores.append(pltpu.make_async_copy(source, outs[i], store_sems.at[i]))
+        stores[-1].start()
+    for store in stores:
+        store.wait()
+
+
+def run_outputs(as_is, rounded, sums, sizes, classes, size):
+    arrays = as_is + rounded
+    out_shape = [jax.ShapeDtypeStruct(a.shape, a.dtype) for a in as_is]
+    out_shape += [jax.ShapeDtypeStruct(a.shape, F32) for a in rounded]
+    out_shape += [jax.ShapeDtypeStruct((length,), F32) for length in sizes.values()]
+    out_shape += [jax.ShapeDtypeStruct((classes, size), F32), jax.ShapeDtypeStruct((classes,), F32)]
+    scratch = [pltpu.VMEM(a.shape, a.dtype) for a in arrays] + [pltpu.VMEM(a.shape, F32) for a in rounded]
+    scratch += [pltpu.SemaphoreType.DMA((len(arrays),))] * 2
+    return pl.pallas_call(
+        functools.partial(outputs_kernel, len(as_is), len(rounded), sizes, classes, size),
+        out_shape=out_shape,
+        in_specs=[ANY] * len(arrays) + [WHOLE],
+        out_specs=[ANY] * len(arrays) + [WHOLE] * (len(sizes) + 2),
+        scratch_shapes=scratch,
+        compiler_params=pltpu.CompilerParams(vmem_limit_bytes=VMEM_BYTES),
+        name="outputs",
+    )(*arrays, sums)
+
+
+def kernel_body(
+    fsdp_size,
+    tokens,
+    in_weight,
+    in_bias,
+    mix_weight,
+    mix_bias,
+    first_gain,
+    first_shift,
+    up_weight,
+    up_bias,
+    down_weight,
+    down_bias,
+    second_gain,
+    second_shift,
+    pool_weight,
+    pool_bias,
+    class_weight,
+    class_bias,
+    lengths,
+    labels,
+    cotangent,
+):
+    layer_out, input_grad, down_grad, up_grad, mix_grad, in_grad, pool_grad, sums = run_layer(
+        fsdp_size,
+        lengths,
+        labels,
+        class_bias,
+        tokens,
+        cotangent,
+        (in_weight, mix_weight, up_weight, down_weight, pool_weight),
+        (in_bias, mix_bias, first_gain, first_shift, up_bias, down_bias, second_gain, second_shift, pool_bias),
+        class_weight.T,
+    )
+    size = mix_bias.shape[0]
+    sizes = {24: 2 * size, 2: size, 3: size, 4: size, 25: 4 * size, 9: size, 10: size, 11: size, 12: size}
+    outs = run_outputs(
+        (layer_out, input_grad, pool_grad),
+        (in_grad, mix_grad, up_grad, down_grad),
+        sums,
+        sizes,
+        class_bias.shape[0],
+        size,
+    )
+    layer_out, input_grad, pool_grad, in_grad, mix_grad, up_grad, down_grad = outs[:7]
+    of_in, of_mix, of_gain_one, of_shift_one, of_up, of_down, of_gain_two, of_shift_two, of_pool = outs[7:16]
+    class_grad, class_bias_grad = outs[16:]
+    return (
+        layer_out,
+        input_grad,
+        in_grad,
+        of_in,
+        mix_grad,
+        of_mix,
+        of_gain_one,
+        of_shift_one,
+        up_grad,
+        of_up,
+        down_grad,
+        of_down,
+        of_gain_two,
+        of_shift_two,
+        pool_grad,
+        of_pool,
+        class_grad.T,
+        class_bias_grad,
+    )
+
+
+def plain_body(
     tokens,
     in_weight,
     in_bias,
@@ -370,4 +1471,6 @@
         P("fsdp", None),
         P(),
     )
+    dp_size, fsdp_size = mesh.shape["dp"], mesh.shape["fsdp"]
+    body = partial(kernel_body, fsdp_size) if (dp_size, fsdp_size) == (4, 8) else plain_body
     return jax.shard_map(body, mesh=mesh, in_specs=in_specs, out_specs=out_specs, check_vma=False)

time: 714 us -> 217 us (0.30); the launches traced: 703 us -> 217 us
  waiting for transfers between devices: 373 us -> 0 us
  Pallas kernels: 0 us -> 215 us
  blocking collectives: 126 us -> 0 us
  matrix products: 103 us -> 0 us
  other arithmetic: 41.2 us -> 0 us
  local copies, waits for them, and re-layouts: 39.3 us -> 0 us
  between operations: 19.6 us -> 2.14 us
    pallas_call x0 -> x2, Pallas kernels: none -> 215 us  [the longest x1 209 us: run_layer(): pl.pallas_call(functools.partial(layer_kernel, fsdp_size), out_shape=out_...]
    reduce_scatter x4 -> x0, waiting for transfers between devices: 201 us -> none  [the longest x1 98 us: body(): lax.psum_scatter(gradients[6], 'fsdp', scatter_dimension=0, tiled=True)]
    dot_general x22 -> x0, matrix products: 103 us -> none  [the longest x1 19.7 us: body(): jnp.dot(first_low, whole_up, preferred_element_type=jnp.float32)]
    unnamed x14 -> x0, waiting for transfers between devices: 81.1 us -> none
    all_gather x5 -> x0, waiting for transfers between devices: 75.8 us -> none  [the longest x1 31.8 us: body(): lax.all_gather(down_weight, 'fsdp', axis=0, tiled=True)]
    psum x2 -> x0, blocking collectives: 52.4 us -> none  [the longest x1 42.1 us: body(): bias_total = lax.psum(grad_class_bias, ('dp', 'fsdp'))]
    unnamed x2 -> x0, blocking collectives: 49.6 us -> none
    unnamed x85 -> x0, local copies, waits for them, and re-layouts: 31.4 us -> none
  transfers between devices with their start and end apart: 12 -> 0, of which waited for: 8 -> 0; matrix products, arithmetic and copies ran while one was open for 20% -> 0% of each run, Pallas kernels for 0% -> 0%
where the time goes in v1:
time: 217 us
  Pallas kernels  215 us (99%)
    pallas_call x1, Pallas kernels, run_layer(): pl.pallas_call(functools.partial(layer_kernel, fsdp_size), out_shape=out_...  209 us
    pallas_call x1, Pallas kernels, run_outputs(): pl.pallas_call(functools.partial(outputs_kernel, len(as_is), len(rounded)...  5.37 us

profile of v1, /device:TPU:8, one launch (start us, length us, event | category | flops | bytes accessed | tf_op | source)
XLA Modules:
  0.0 216.9 jit_solution(6596590745755587843)
XLA Ops:
  2.0 209.3 %layer.1 = (bf16[512,768]{1,0:T(8,128)(2,1)}, f32[512,768]{1,0:T(8,128)}, bf16[384,768]{1,0:T(8,128)(2,1)}, bf16[96,3072]{1,0:T(8,128)(2,1)}, bf16[96,768]{1,0:T...) custom-call(s32[1]{0:T(128)S(6)} %copy.38.refs_0_, s32[1]{0:T(128)S(6)} %copy.39.refs_1_, ...), custom_call_target="tpu_custom_call" | custom-call | tf_op jit(solution)/shard_map/layer/pallas_call | solution.py:1004
  211.3 5.4 %outputs.1 = (bf16[512,768]{1,0:T(8,128)(2,1)}, f32[512,768]{1,0:T(8,128)}, f32[96,768]{1,0:T(8,128)}, f32[96,2304]{1,0:T(8,128)}, f32[96,768]{1,0:T(8,128)}, /*...) custom-call(bf16[512,768]{1,0:T(8,128)(2,1)} %get-tuple-element.44.r, ...), custom_call_target="tpu_custom_call" | custom-call | tf_op jit(solution)/shard_map/outputs/pallas_call | solution.py:1057

commit v2 on v1

--- a/solution.py
+++ b/solution.py
@@ -109,9 +109,8 @@
         ]
 
     def go(self, index, src, dst, target):
-        copy = remote(src, dst, self.send_sems.at[index], self.recv_sems.at[index], target)
-        copy.start()
-        self.started.append(copy)
+        remote(src, dst, self.send_sems.at[index], self.recv_sems.at[index], target).start()
+        self.started.append((index, dst.shape[-2:]))
 
     def arrived(self, index, dst):
         remote(dst, dst, self.send_sems.at[index], self.recv_sems.at[index], self.place.partner()).wait_recv()
@@ -126,8 +125,12 @@
         for hop in range(1, p.line):
             self.go(hop - 1, piece, self.quarter(p.shard, p.row_half, p.col_half), p.on_line(hop))
         self.go(4 * self.hops, self.shard_ref, self.block(p.shard), p.partner())
-        self.own = pltpu.make_async_copy(self.shard_ref, self.block(p.shard), self.recv_sems.at[5 * self.hops + 1])
-        self.own.start()
+        self.own().start()
+
+    def own(self):
+        return pltpu.make_async_copy(
+            self.shard_ref, self.block(self.place.shard), self.recv_sems.at[5 * self.hops + 1]
+        )
 
     def source(self, hop):
         return 2 * self.place.source_spot(hop) + self.place.core
@@ -154,14 +157,15 @@
 
     def ready(self):
         p = self.place
-        self.own.wait()
+        self.own().wait()
         self.arrived(4 * self.hops, self.block(p.shard + 1 - 2 * p.core))
         for hop in range(1, p.line):
             self.arrived(4 * self.hops + hop, self.block(2 * p.source_spot(hop) + 1 - p.core))
 
     def end(self):
-        for copy in self.started:
-            copy.wait_send()
+        for index, (rows, cols) in self.started:
+            like = self.whole.at[0, 0, pl.ds(0, rows), pl.ds(0, cols)]
+            remote(like, like, self.send_sems.at[index], self.recv_sems.at[index], self.place.partner()).wait_send()
 
 
 class SmallGather:
@@ -171,6 +175,10 @@
         self.hops = place.line - 1
         self.started = []
 
+    def at(self, shard):
+        rows, cols = self.own_ref.shape
+        return self.all.at[pl.ds(pl.multiple_of(shard * rows, rows), rows), pl.ds(0, cols)]
+
     @staticmethod
     def sems(line):
         return 2 * (line - 1) + 2
@@ -186,24 +194,24 @@
     def begin(self):
         p = self.place
         for hop in range(1, p.line):
-            self.go(hop - 1, self.own_ref, self.all.at[p.shard], p.on_line(hop))
-        self.go(2 * self.hops, self.own_ref, self.all.at[p.shard], p.partner())
-        self.own = pltpu.make_async_copy(self.own_ref, self.all.at[p.shard], self.recv_sems.at[2 * self.hops + 1])
+            self.go(hop - 1, self.own_ref, self.at(p.shard), p.on_line(hop))
+        self.go(2 * self.hops, self.own_ref, self.at(p.shard), p.partner())
+        self.own = pltpu.make_async_copy(self.own_ref, self.at(p.shard), self.recv_sems.at[2 * self.hops + 1])
         self.own.start()
 
     def hand(self):
         p = self.place
         for hop in range(1, p.line):
-            block = self.all.at[2 * p.source_spot(hop) + p.core]
+            block = self.at(2 * p.source_spot(hop) + p.core)
             self.arrived(hop - 1, block)
             self.go(self.hops + hop - 1, block, block, p.partner())
 
     def ready(self):
         p = self.place
         self.own.wait()
-        self.arrived(2 * self.hops, self.all.at[p.shard + 1 - 2 * p.core])
+        self.arrived(2 * self.hops, self.at(p.shard + 1 - 2 * p.core))
         for hop in range(1, p.line):
-            self.arrived(self.hops + hop - 1, self.all.at[2 * p.source_spot(hop) + 1 - p.core])
+            self.arrived(self.hops + hop - 1, self.at(2 * p.source_spot(hop) + 1 - p.core))
 
     def end(self):
         for copy in self.started:
@@ -217,7 +225,6 @@
         self.from_line, self.done = from_line, done
         self.send_sems, self.recv_sems = send_sems, recv_sems
         self.line, _, self.rows, self.cols = grad.shape
-        self.started = []
 
     @staticmethod
     def sems(line):
@@ -235,9 +242,7 @@
         ]
 
     def go(self, index, src, dst, target):
-        copy = remote(src, dst, self.send_sems.at[index], self.recv_sems.at[index], target)
-        copy.start()
-        self.started.append(copy)
+        remote(src, dst, self.send_sems.at[index], self.recv_sems.at[index], target).start()
 
     def arrived(self, index, dst):
         remote(dst, dst, self.send_sems.at[index], self.recv_sems.at[index], self.place.partner()).wait_recv()
@@ -251,8 +256,8 @@
 
     def halves(self, side, which):
         p = self.place
-        row_half = jnp.where(p.core == 0, which, side)
-        col_half = jnp.where(p.core == 0, side, which)
+        row_half = which * (1 - p.core) + side * p.core
+        col_half = side * (1 - p.core) + which * p.core
         return self.slices(row_half, col_half)
 
     def swap(self):
@@ -262,7 +267,7 @@
     def add(self, rows, cols, others, targets_spot=None):
         p = self.place
         half_rows, half_cols = self.rows // 2, self.cols // 2
-        step = 48 if half_rows % 48 == 0 else 16
+        step = next(size for size in (64, 48, 32, 16) if half_rows % size == 0)
         steps = half_rows // step
 
         def one(index, carry):
@@ -337,8 +342,14 @@
             self.arrived(2 + self.line + step, self.done.at[other // 2, lax.rem(other, 2)])
 
     def end(self):
-        for copy in self.started:
-            copy.wait_send()
+        third = 2 + self.line
+        landed = {0: self.from_core, 1: self.from_first.at[0], 2: self.from_first.at[0], 3: self.from_second}
+        for hop in range(1, self.line):
+            landed[3 + hop] = self.from_line.at[0]
+        for step in range(1, 4):
+            landed[third + step] = self.done.at[0, 0]
+        for index, like in landed.items():
+            remote(like, like, self.send_sems.at[index], self.recv_sems.at[index], self.place.partner()).wait_send()
 
 
 class SmallSum:
@@ -413,9 +424,8 @@
         return 3 + (line - 1) + line
 
     def go(self, index, ref, target):
-        copy = remote(ref, ref, self.send_sems.at[index], self.recv_sems.at[index], target)
-        copy.start()
-        self.started.append(copy)
+        remote(ref, ref, self.send_sems.at[index], self.recv_sems.at[index], target).start()
+        self.started.append((index, len(ref.shape)))
 
     def arrived(self, index, dst):
         remote(dst, dst, self.send_sems.at[index], self.recv_sems.at[index], self.place.partner()).wait_recv()
@@ -448,12 +458,14 @@
             self.arrived(2 + p.line + hop, self.blocks.at[2 * p.source_spot(hop) + 1 - p.core])
 
     def end(self):
-        for copy in self.started:
-            copy.wait_send()
+        for index, rank in self.started:
+            like = self.blocks.at[0] if rank == 3 else self.blocks.at[0, 0]
+            remote(like, like, self.send_sems.at[index], self.recv_sems.at[index], self.place.partner()).wait_send()
 ANY = pl.BlockSpec(memory_space=pl.ANY)
 WHOLE = pl.BlockSpec(memory_space=pltpu.VMEM)
 SCALARS = pl.BlockSpec(memory_space=pltpu.SMEM)
-VMEM_BYTES = 67_000_000
+VMEM_BYTES = 67_043_328
+AHEAD = 4
 BF16, F32 = jnp.bfloat16, jnp.float32
 
 
@@ -548,16 +560,17 @@
     shards = take(5)
     vectors, class_rows = take(9), take(1)[0]
     layer_out, input_grad, down_out, up_out, mix_out, in_out, pool_out, sums_out = take(8)
-    w_in, w_mix, w_up, w_down, w_pool, small_all = take(6)
+    w_in, w_mix, w_up, w_down, w_pool = take(5)
     g_down, g_up = take(2)
-    recv = [take(5) for _ in range(4)]
+    recv = [take(5) for _ in range(7)]
+    recv.append([recv[1][0].at[:, pl.ds(0, shards[0].shape[0]), :]] + take(4))
     sum_refs = take(4)
     (blocks,) = take(1)
     tok, tok_t, cot, att, att_t, first, first_t = take(7)
     qkv, act, slope = take(3)
     unit_one, unit_two, grad = take(3)
     inv_one, inv_two, key_mask, lse, vec = take(5)
-    short, small_in, bias_row, sums_all = take(4)
+    short, small_in, bias_row = take(3)
     g_send, g_recv, s_send, s_recv, q_send, q_recv, v_send, v_recv, b_send, b_recv, local = take(11)
     seq, width = tok.shape
     hidden = act.shape[1]
@@ -578,17 +591,34 @@
     classes = class_bias.shape[0]
     bias_row[0:1, 13 : 13 + classes] = class_bias[...].astype(F32).reshape(1, classes)
     place.meet()
-    gathers = [
-        Gather(place, shard, whole, g_send.at[i], g_recv.at[i])
-        for i, (shard, whole) in enumerate(zip(shards, (w_in, w_mix, w_up, w_down, w_pool)))
-    ]
-    for_in, for_mix, for_up, for_down, for_pool = gathers
-    little = SmallGather(place, small_in, small_all, v_send, v_recv)
-    for_in.begin()
+    everything, all_rows = [], shards[0].shape[0]
+    for shard, whole in zip(shards, (w_in, w_mix, w_up, w_down, w_pool)):
+        for row in range(0, shard.shape[0], all_rows):
+            for col in range(0, shard.shape[1], width):
+                rows, cols = pl.ds(row, all_rows), pl.ds(col, width)
+                everything.append((shard.at[rows, cols], whole.at[:, :, rows, cols]))
+    gathers = [Gather(place, *pair, g_send.at[i], g_recv.at[i]) for i, pair in enumerate(everything)]
+    little = SmallGather(place, small_in, slope, v_send, v_recv)
+    hops = range(1, line)
+    first_mix, first_up, first_down, first_pool = 3, 4, 4 + parts, 4 + 2 * parts
+
+    def tick(count):
+        if count + AHEAD < len(gathers):
+            gathers[count + AHEAD].begin()
+        if count < len(gathers):
+            for hop in hops:
+                gathers[count].spread(hop)
+        if 0 <= count - 1 < len(gathers):
+            for hop in hops:
+                gathers[count - 1].relay(hop)
+        if 0 <= count - 2 < len(gathers):
+            for hop in hops:
+                gathers[count - 2].hand(hop)
+
+    gathers[0].begin()
     little.begin()
-    for one in gathers[1:]:
+    for one in gathers[1:AHEAD]:
         one.begin()
-    hops = range(1, line)
     length = lengths[0]
     label = labels[0]
 
@@ -606,23 +636,16 @@
     loop(seq // 128, mask_cot)
     grad_low = cot
 
-    for hop in hops:
-        for_in.spread(hop)
+    tick(0)
     little.hand()
-    for hop in hops:
-        for_in.relay(hop)
-    for hop in hops:
-        for_mix.spread(hop)
+    tick(1)
     little.ready()
-    vec[...] = jnp.sum(small_all[...].astype(F32), axis=0)
-    for hop in hops:
-        for_in.hand(hop)
-    for hop in hops:
-        for_mix.relay(hop)
-    for_in.ready()
+    vec[...] = jnp.sum(slope[0 : 16 * fsdp_size, 0:width].reshape(fsdp_size, 16, width).astype(F32), axis=0)
 
     score_scale = 1.0 / math.sqrt(DH)
     for part in range(3):
+        tick(2 + part)
+        gathers[part].ready()
 
         def project(index, part=part):
             inner = lanes(index * 256, 256)
@@ -637,8 +660,6 @@
             qkv[:, cols] = out
 
         loop(width // 256, project)
-    for hop in hops:
-        for_mix.hand(hop)
 
     low_lanes = lax.broadcasted_iota(jnp.int32, (1, 128), 1) < 64
     zero_low = jnp.zeros((), BF16)
@@ -666,21 +687,18 @@
         att_t[rows_of(pl.multiple_of(pair * 128, 128), 128), :] = both.astype(BF16)
         att[:, lanes(pair * 128, 128)] = both.T.astype(BF16)
 
-    def attend_some(first_pair, last_pair):
-        lax.fori_loop(first_pair, last_pair, lambda pair, carry: (attend(pair), carry)[1], 0)
-
-    attend_some(0, 2)
-    for hop in hops:
-        for_up.spread(hop)
-    attend_some(2, 4)
-    for hop in hops:
-        for_up.relay(hop)
-    attend_some(4, pairs)
-    for hop in hops:
-        for_down.spread(hop)
-    for hop in hops:
-        for_up.hand(hop)
-    for_mix.ready()
+    def attend_on(pair):
+        attend(pair)
+        for one in range(pairs):
+
+            @pl.when(pair == one)
+            def _(one=one):
+                tick(5 + one)
+
+    loop(pairs, attend_on)
+    gathers[first_mix].ready()
+
+    little.end()
 
     gain_one, shift_one = vec[3:4, :], vec[4:5, :]
 
@@ -699,13 +717,10 @@
 
     loop(seq // 256, norm_one)
     first_t[...] = first[...].T
-    for hop in hops:
-        for_down.relay(hop)
-    for hop in hops:
-        for_pool.spread(hop)
-    for_up.ready()
+    tick(5 + pairs)
 
     for part in range(parts):
+        gathers[first_up + part].ready()
 
         def raise_up(index, part=part):
             inner = lanes(index * 384, 384)
@@ -716,15 +731,10 @@
             slope[:, cols] = derivative.astype(BF16)
 
         loop(width // 384, raise_up)
-        if part == 0:
-            for hop in hops:
-                for_down.hand(hop)
-        if part == 1:
-            for hop in hops:
-                for_pool.relay(hop)
-    for hop in hops:
-        for_pool.hand(hop)
-    for_down.ready()
+        if part < 3:
+            tick(6 + pairs + part)
+    for one in gathers[first_down:first_pool]:
+        one.ready()
     gain_two, shift_two = vec[10:11, :], vec[11:12, :]
 
     def norm_two(index):
@@ -742,7 +752,7 @@
     stores = [pltpu.make_async_copy(att, layer_out, local.at[2])]
     stores[0].start()
 
-    for_pool.ready()
+    gathers[first_pool].ready()
     top = lax.broadcasted_iota(jnp.int32, (16, 1), 0) == 0
     head = att[0:16, :]
     vec_low = vec[...].astype(BF16)
@@ -769,9 +779,6 @@
     sequences.begin()
     grad[0:16, :] += nt(grad_pool_pre, w_pool[...].reshape(width, width))
 
-    for one in gathers:
-        one.end()
-
     def norm_back(unit_ref, inv_ref, gain, gain_row, shift_row, bias_row, size):
         def one(index, carry):
             by_gain, by_shift, by_bias = carry
@@ -798,19 +805,24 @@
 
     norm_back(unit_two, inv_two, gain_two, 10, 11, 9, 128)
 
-    scatters = [
-        Scatter(place, ref, *recv[i], s_send.at[i], s_recv.at[i])
-        for i, ref in enumerate((g_down, g_up, w_up.at[:, :, :, pl.ds(3 * width, width)], w_up.at[:, :, :, pl.ds(0, 3 * width)]))
-    ]
-    of_down, of_up, of_mix, of_in = scatters
     rows_down = hidden // fsdp_size
-
-    def down_gradient(index):
-        cols = lanes(index * rows_down, rows_down)
-        g_down[index // 2, lax.rem(index, 2)] = tn(act[:, cols], grad_low[...]).astype(BF16)
-
-    loop(fsdp_size, down_gradient)
-    of_down.swap()
+    few = 128
+    many = rows_down - few
+    pieces = [g_down.at[:, :, pl.ds(many, few), :], g_down.at[:, :, pl.ds(0, many), :]]
+    pieces += [g_up.at[:, :, :, pl.ds(half * 2 * width, 2 * width)] for half in (0, 1)]
+    pieces += [w_up.at[:, :, :, pl.ds(at * width, width)] for at in (3, 0, 1, 2)]
+    scatters = [Scatter(place, ref, *recv[i], s_send.at[i], s_recv.at[i]) for i, ref in enumerate(pieces)]
+    down_a, down_b, up_a, up_b, of_mix, in_a, in_b, in_c = scatters
+
+    for first_row, count, one in ((many, few, down_a), (0, many, down_b)):
+
+        def down_gradient(index, first_row=first_row, count=count):
+            cols = lanes(index * rows_down + first_row, count)
+            out = tn(act[:, cols], grad_low[...]).astype(BF16)
+            g_down[index // 2, lax.rem(index, 2), pl.ds(first_row, count), :] = out
+
+        loop(fsdp_size, down_gradient)
+        one.swap()
     sequences.to_line()
 
     for part in range(parts):
@@ -824,18 +836,26 @@
             sums[5 + part : 6 + part, inner] = jnp.sum(low.astype(F32), axis=0, keepdims=True)
 
         loop(2, through_down)
+
+        def up_gradient(index, part=part):
+            cols = lanes(part * width + index * 256, 256)
+            out = nn(first_t[...], slope[:, cols]).astype(BF16)
+            g_up[:, :, :, cols] = out.reshape(line, 2, width // fsdp_size, 256)
+
+        loop(width // 256, up_gradient)
+        if part == 0:
+            down_a.to_first()
         if part == 1:
-            of_down.to_first()
-
-    def up_gradient(index):
-        cols = lanes(index * 256, 256)
-        out = nn(first_t[...], slope[:, cols]).astype(BF16)
-        g_up[:, :, :, cols] = out.reshape(line, 2, width // fsdp_size, 256)
-
-    loop(hidden // 256, up_gradient)
-    of_up.swap()
-    of_down.to_second()
-    sequences.hand()
+            up_a.swap()
+            down_b.to_first()
+            down_a.to_second()
+        if part == 2:
+            up_a.to_first()
+            down_a.to_line()
+        if part == 3:
+            up_b.swap()
+            down_b.to_second()
+            sequences.hand()
 
     half_line = line // 2
     half_width = width // 2
@@ -844,11 +864,21 @@
         cols = lanes(index * half_width, half_width)
         weight = w_up[rows_of(index * half_line, half_line)].reshape(half_width, hidden)
         grad[:, cols] += nt(slope[...], weight)
+        for one in (0, 1):
+
+            @pl.when(index == one)
+            def _(one=one):
+                if one == 0:
+                    up_b.to_first()
+                    down_b.to_line()
+                else:
+                    up_a.to_second()
+                    down_a.to_plane()
 
     loop(2, through_up)
-    of_up.to_first()
-    of_down.to_line()
     norm_back(unit_one, inv_one, gain_one, 3, 4, 2, 128)
+    for one in gathers:
+        one.end()
 
     def mix_gradient(index):
         out = nn(att_t[...], grad_low[:, lanes(index * 256, 256)]).astype(BF16)
@@ -856,6 +886,7 @@
 
     loop(width // 256, mix_gradient)
     of_mix.swap()
+    up_b.to_second()
 
     def through_mix(index):
         cols = lanes(index * half_width, half_width)
@@ -863,7 +894,8 @@
         first[:, cols] = nt(grad_low[...], weight).astype(BF16)
 
     loop(2, through_mix)
-    of_up.to_second()
+    of_mix.to_first()
+    up_a.to_line()
 
     def attend_back(pair):
         at = [lanes(part * width + pair * 128, 128) for part in range(3)]
@@ -887,55 +919,69 @@
         qkv[:, at[1]] = by_key.astype(BF16)
         qkv[:, at[2]] = by_value.astype(BF16)
 
-    def attend_back_some(first_pair, last_pair):
-        lax.fori_loop(first_pair, last_pair, lambda pair, carry: (attend_back(pair), carry)[1], 0)
-
-    attend_back_some(0, 1)
-    of_mix.to_first()
-    of_down.to_plane()
-    attend_back_some(1, 2)
-    of_up.to_line()
-    attend_back_some(2, 3)
-    of_mix.to_second()
-    attend_back_some(3, 4)
-    sequences.ready()
-    attend_back_some(4, 5)
-    of_up.to_plane()
-    of_mix.to_line()
-    attend_back_some(5, pairs)
-
-    for part in range(3):
-
-        def in_gradient(index, part=part):
-            inner = lanes(index * 256, 256)
-            cols = lanes(part * width + index * 256, 256)
-            incoming = qkv[:, cols]
-            w_up[:, :, :, cols] = nn(tok_t[...], incoming).astype(BF16).reshape(line, 2, width // fsdp_size, 256)
+    after_pair = {
+        0: [down_b.to_plane],
+        1: [up_b.to_line, of_mix.to_second],
+        2: [in_a.to_first, up_a.to_plane],
+        3: [of_mix.to_line, in_a.to_second],
+        4: [in_b.to_first, up_b.to_plane],
+        5: [in_a.to_line, of_mix.to_plane, in_b.to_second],
+    }
+
+    def attend_back_on(pair):
+        attend_back(pair)
+        for one in range(pairs):
+
+            @pl.when(pair == one)
+            def _(one=one):
+                for step in after_pair[one]:
+                    step()
+
+    def in_gradient(chunk):
+        for part in range(3):
+            inner = lanes(chunk * 256, 256)
+            incoming = qkv[:, lanes(part * width + chunk * 256, 256)]
+            out = nn(tok_t[...], incoming).astype(BF16).reshape(line, 2, width // fsdp_size, 256)
+            w_up[:, :, :, lanes(chunk * width + part * 256, 256)] = out
             if part != 1:
                 row = 0 if part == 0 else 1
                 sums[row : row + 1, inner] = jnp.sum(incoming.astype(F32), axis=0, keepdims=True)
 
-        loop(width // 256, in_gradient)
-    of_in.swap()
+    def attend_chunk(chunk):
+        lax.fori_loop(2 * chunk, 2 * chunk + 2, lambda pair, carry: (attend_back_on(pair), carry)[1], 0)
+        in_gradient(chunk)
+        for at, one in enumerate((in_a, in_b, in_c)):
+
+            @pl.when(chunk == at)
+            def _(one=one):
+                one.swap()
+
+    loop(pairs // 2, attend_chunk)
+    sequences.ready()
     total = SmallSum(place, *sum_refs, b_send, b_recv)
     total.swap()
-    of_mix.to_plane()
 
     def through_in(index):
         cols = lanes(index * half_width, half_width)
         weight = w_in[rows_of(index * half_line, half_line)].reshape(half_width, 3 * width)
         grad[:, cols] += nt(qkv[...], weight)
-
-    loop(1, through_in)
-    of_in.to_first()
-    total.to_line()
-    loop_from_one = lambda step: lax.fori_loop(1, 2, lambda index, carry: (step(index), carry)[1], 0)
-    loop_from_one(through_in)
+        for one in (0, 1):
+
+            @pl.when(index == one)
+            def _(one=one):
+                if one == 0:
+                    in_c.to_first()
+                    in_b.to_line()
+                else:
+                    in_a.to_plane()
+
+    loop(2, through_in)
     store = pltpu.make_async_copy(grad, input_grad, local.at[3])
     store.start()
     stores.append(store)
-    of_in.to_second()
-    total.to_plane()
+    in_c.to_second()
+    total.to_line()
+    in_b.to_plane()
 
     every = blocks[...].reshape(fsdp_size * 4 * 16, width)
     count = fsdp_size * 4 * 16
@@ -948,24 +994,45 @@
     own_part = nt(pick, every).astype(BF16)
     pool_out[...] = nn(own_part, paired)[0 : width // fsdp_size, :]
 
-    of_in.to_line()
-    total.finish(sums_all)
-    own_sums(place.shard, fsdp_size, sums_all, sums_out, classes)
-    of_in.to_plane()
-    for index, (one, out) in enumerate(zip(scatters, (down_out, up_out, mix_out, in_out))):
+    in_c.to_line()
+    total.to_plane()
+
+    wide = 256
+    kept = [
+        (down_a, down_out, many, [(0, 0, width)]),
+        (down_b, down_out, 0, [(0, 0, width)]),
+        (up_a, up_out, 0, [(0, 0, 2 * width)]),
+        (up_b, up_out, 0, [(0, 2 * width, 2 * width)]),
+        (of_mix, mix_out, 0, [(0, 0, width)]),
+    ]
+    for chunk, one in enumerate((in_a, in_b, in_c)):
+        kept.append((one, in_out, 0, [(part * wide, part * width + chunk * wide, wide) for part in range(3)]))
+
+    def keep(one, out, first_row, spans):
         one.finish()
         half_rows, half_cols = one.rows // 2, one.cols // 2
-        for quarter in range(4):
-            row_half, col_half = quarter // 2, quarter % 2
-            target = out.at[
-                pl.ds(row_half * half_rows, half_rows), pl.ds(col_half * half_cols, half_cols)
-            ]
-            store = pltpu.make_async_copy(one.done.at[row_half, col_half], target, local.at[4 + 4 * index + quarter])
-            store.start()
-            stores.append(store)
+        for row_half in (0, 1):
+            rows = pl.ds(first_row + row_half * half_rows, half_rows)
+            for col_half in (0, 1):
+                begin, end = col_half * half_cols, (col_half + 1) * half_cols
+                for here, there, count in spans:
+                    low, high = max(here, begin), min(here + count, end)
+                    if low < high:
+                        source = one.done.at[row_half, col_half, :, pl.ds(low - begin, high - low)]
+                        target = out.at[rows, pl.ds(there + low - here, high - low)]
+                        store = pltpu.make_async_copy(source, target, local.at[len(stores) + 2])
+                        store.start()
+                        stores.append(store)
+
+    for item in kept[:-1]:
+        keep(*item)
+    total.finish(total.from_core)
+    own_sums(place.shard, fsdp_size, total.from_core, sums_out, classes)
+    in_c.to_plane()
+    keep(*kept[-1])
     for store in stores:
         store.wait()
-    for one in scatters + [little, sequences, total]:
+    for one in scatters + [sequences, total]:
         one.end()
 
 
@@ -976,10 +1043,14 @@
     hidden = up_shard.shape[1]
     vmem, dma = pltpu.VMEM, pltpu.SemaphoreType.DMA
     reduced = (down_shard, up_shard, mix_shard, in_shard)
-    scratch = [vmem((line, 2) + s.shape, BF16) for s in shards] + [vmem((fsdp_size, 16, width), BF16)]
+    block = width // fsdp_size
+    few = 128
+    sizes = [(few, width), (down_shard.shape[0] - few, width)] + [(block, 2 * width)] * 2 + [(block, width)] * 4
+    scratch = [vmem((line, 2) + s.shape, BF16) for s in shards]
     scratch += [vmem((line, 2) + s.shape, BF16) for s in (down_shard, up_shard)]
-    for s in reduced:
-        scratch += Scatter.scratch(line, *s.shape)
+    for size in sizes:
+        scratch += Scatter.scratch(line, *size)
+    del scratch[-5]
     scratch += SmallSum.scratch(line, 24, width)
     scratch += [vmem((fsdp_size, 4, 16, width), BF16)]
     rows, turned = vmem((seq, width), BF16), vmem((width, seq), BF16)
@@ -988,16 +1059,16 @@
     scratch += [vmem((seq, width), F32)] * 3
     scratch += [vmem((seq, 128), F32)] * 3 + [vmem((width // 128, 8, seq), F32), vmem((16, width), F32)]
     span = hidden // fsdp_size
-    scratch += [vmem((16, span), F32), vmem((16, width), BF16), vmem((8, 128), F32), vmem((24, width), F32)]
+    scratch += [vmem((16, span), F32), vmem((16, width), BF16), vmem((8, 128), F32)]
     for count in (
-        (5, Gather.sems(line)),
-        (4, Scatter.sems(line)),
+        (sum(s.shape[0] * s.shape[1] for s in shards) // (block * width), Gather.sems(line)),
+        (len(sizes), Scatter.sems(line)),
         (SequenceGather.sems(line),),
         (SmallGather.sems(line),),
         (SmallSum.sems(line),),
     ):
         scratch += [dma(count), dma(count)]
-    scratch += [dma((20,))]
+    scratch += [dma((64,))]
     out_shape = [jax.ShapeDtypeStruct((seq, width), BF16), jax.ShapeDtypeStruct((seq, width), F32)]
     out_shape += [jax.ShapeDtypeStruct(s.shape, BF16) for s in reduced]
     out_shape += [jax.ShapeDtypeStruct((width // fsdp_size, width), F32), jax.ShapeDtypeStruct((32, span), F32)]

time: 217 us -> 199 us (0.917)
  Pallas kernels: 215 us -> 195 us
    pallas_call x1, Pallas kernels: 209 us -> 189 us  [run_layer(): pl.pallas_call(functools.partial(layer_kernel, fsdp_size), out_shape=out_...]
where the time goes in v2:
time: 199 us; the launch traced here: 197 us
  Pallas kernels  195 us (98%)
  between operations  2.12 us (1%)
    pallas_call x1, Pallas kernels, run_layer(): pl.pallas_call(functools.partial(layer_kernel, fsdp_size), out_shape=out_...  189 us
    pallas_call x1, Pallas kernels, run_outputs(): pl.pallas_call(functools.partial(outputs_kernel, len(as_is), len(rounded)...  5.37 us

profile of v2, /device:TPU:8, one launch (start us, length us, event | category | flops | bytes accessed | tf_op | source)
XLA Modules:
  0.0 196.7 jit_solution(14742703070415009735)
XLA Ops:
  2.0 189.2 %layer.1 = (bf16[512,768]{1,0:T(8,128)(2,1)}, f32[512,768]{1,0:T(8,128)}, bf16[384,768]{1,0:T(8,128)(2,1)}, bf16[96,3072]{1,0:T(8,128)(2,1)}, bf16[96,768]{1,0:T...) custom-call(s32[1]{0:T(128)S(6)} %copy.38.refs_0_, s32[1]{0:T(128)S(6)} %copy.39.refs_1_, ...), custom_call_target="tpu_custom_call" | custom-call | tf_op jit(solution)/shard_map/layer/pallas_call | solution.py:1075
  191.2 5.4 %outputs.1 = (bf16[512,768]{1,0:T(8,128)(2,1)}, f32[512,768]{1,0:T(8,128)}, f32[96,768]{1,0:T(8,128)}, f32[96,2304]{1,0:T(8,128)}, f32[96,768]{1,0:T(8,128)}, /*...) custom-call(bf16[512,768]{1,0:T(8,128)(2,1)} %get-tuple-element.44.r, ...), custom_call_target="tpu_custom_call" | custom-call | tf_op jit(solution)/shard_map/outputs/pallas_call | solution.py:1128

commit v3 on v2

--- a/solution.py
+++ b/solution.py
@@ -348,6 +348,95 @@
             landed[3 + hop] = self.from_line.at[0]
         for step in range(1, 4):
             landed[third + step] = self.done.at[0, 0]
+        for index, like in landed.items():
+            remote(like, like, self.send_sems.at[index], self.recv_sems.at[index], self.place.partner()).wait_send()
+
+
+class LineFirst(Scatter):
+    def __init__(self, place, grad, from_core, from_line, from_plane, done, send_sems, recv_sems):
+        self.place, self.grad = place, grad
+        self.from_core, self.from_line, self.from_plane, self.done = from_core, from_line, from_plane, done
+        self.send_sems, self.recv_sems = send_sems, recv_sems
+        self.line, _, self.rows, self.cols = grad.shape
+
+    @staticmethod
+    def scratch(line, rows, cols):
+        half = (rows // 2, cols // 2)
+        return [
+            pltpu.VMEM((line, rows, cols), jnp.bfloat16),
+            pltpu.VMEM((line - 1, rows, cols), jnp.bfloat16),
+            pltpu.VMEM((3,) + half, jnp.bfloat16),
+            pltpu.VMEM((2, 2) + half, jnp.bfloat16),
+        ]
+
+    def quarter(self, dp):
+        rows, cols = self.slices(dp // 2, lax.rem(dp, 2))
+        return self.grad.at[self.place.spot, self.place.core, rows, cols]
+
+    def to_first(self):
+        p = self.place
+        self.arrived(0, self.from_core)
+        step = 32
+        steps = self.rows // step
+
+        def one(index, carry):
+            spot, at = index // steps, pl.ds(pl.multiple_of(lax.rem(index, steps) * step, step), step)
+            total = self.grad[spot, p.core, at, :].astype(jnp.float32) + self.from_core[spot, at, :].astype(jnp.float32)
+            self.grad[spot, p.core, at, :] = total.astype(jnp.bfloat16)
+            return carry
+
+        lax.fori_loop(0, self.line * steps, one, 0)
+        for hop in range(1, self.line):
+            spot = lax.rem(p.spot + hop, self.line)
+            self.go(hop, self.grad.at[spot, p.core], self.from_line.at[hop - 1], p.on_line(hop))
+
+    def to_second(self):
+        p = self.place
+        for hop in range(1, self.line):
+            self.arrived(hop, self.from_line.at[hop - 1])
+        step = 32
+
+        def one(part, carry):
+            at = pl.ds(pl.multiple_of(part * step, step), step)
+            total = self.grad[p.spot, p.core, at, :].astype(jnp.float32)
+            for hop in range(1, self.line):
+                total = total + self.from_line[hop - 1, at, :].astype(jnp.float32)
+            self.grad[p.spot, p.core, at, :] = total.astype(jnp.bfloat16)
+            return carry
+
+        lax.fori_loop(0, self.rows // step, one, 0)
+        for step in range(1, 4):
+            other = lax.rem(p.dp + step, 4)
+            self.go(self.line - 1 + step, self.quarter(other), self.from_plane.at[step - 1], p.in_plane(other))
+
+    def to_line(self):
+        p = self.place
+        for step in range(1, 4):
+            self.arrived(self.line - 1 + step, self.from_plane.at[step - 1])
+        rows, cols = self.slices(p.row_half, p.col_half)
+        size = 16
+
+        def one(part, carry):
+            at = pl.ds(pl.multiple_of(rows.start + part * size, 16), size)
+            inner = pl.ds(pl.multiple_of(part * size, 16), size)
+            total = self.grad[p.spot, p.core, at, cols].astype(jnp.float32)
+            for step in range(3):
+                total = total + self.from_plane[step, inner, :].astype(jnp.float32)
+            self.done[p.row_half, p.col_half, inner, :] = total.astype(jnp.bfloat16)
+            return carry
+
+        lax.fori_loop(0, self.rows // 2 // size, one, 0)
+        own = self.done.at[p.row_half, p.col_half]
+        for step in range(1, 4):
+            self.go(2 + self.line + step, own, own, p.in_plane(lax.rem(p.dp + step, 4)))
+
+    def end(self):
+        landed = {0: self.from_core}
+        for hop in range(1, self.line):
+            landed[hop] = self.from_line.at[0]
+        for step in range(1, 4):
+            landed[self.line - 1 + step] = self.from_plane.at[0]
+            landed[2 + self.line + step] = self.done.at[0, 0]
         for index, like in landed.items():
             remote(like, like, self.send_sems.at[index], self.recv_sems.at[index], self.place.partner()).wait_send()
 
@@ -562,7 +651,7 @@
     layer_out, input_grad, down_out, up_out, mix_out, in_out, pool_out, sums_out = take(8)
     w_in, w_mix, w_up, w_down, w_pool = take(5)
     g_down, g_up = take(2)
-    recv = [take(5) for _ in range(7)]
+    recv = [take(4)] + [take(5) for _ in range(6)]
     recv.append([recv[1][0].at[:, pl.ds(0, shards[0].shape[0]), :]] + take(4))
     sum_refs = take(4)
     (blocks,) = take(1)
@@ -605,15 +694,15 @@
     def tick(count):
         if count + AHEAD < len(gathers):
             gathers[count + AHEAD].begin()
+        if 0 <= count - 3 < len(gathers):
+            for hop in hops:
+                gathers[count - 3].hand(hop)
         if count < len(gathers):
             for hop in hops:
                 gathers[count].spread(hop)
         if 0 <= count - 1 < len(gathers):
             for hop in hops:
                 gathers[count - 1].relay(hop)
-        if 0 <= count - 2 < len(gathers):
-            for hop in hops:
-                gathers[count - 2].hand(hop)
 
     gathers[0].begin()
     little.begin()
@@ -639,12 +728,13 @@
     tick(0)
     little.hand()
     tick(1)
+    tick(2)
     little.ready()
     vec[...] = jnp.sum(slope[0 : 16 * fsdp_size, 0:width].reshape(fsdp_size, 16, width).astype(F32), axis=0)
 
     score_scale = 1.0 / math.sqrt(DH)
     for part in range(3):
-        tick(2 + part)
+        tick(3 + part)
         gathers[part].ready()
 
         def project(index, part=part):
@@ -693,7 +783,7 @@
 
             @pl.when(pair == one)
             def _(one=one):
-                tick(5 + one)
+                tick(6 + one)
 
     loop(pairs, attend_on)
     gathers[first_mix].ready()
@@ -717,7 +807,7 @@
 
     loop(seq // 256, norm_one)
     first_t[...] = first[...].T
-    tick(5 + pairs)
+    tick(6 + pairs)
 
     for part in range(parts):
         gathers[first_up + part].ready()
@@ -732,7 +822,7 @@
 
         loop(width // 384, raise_up)
         if part < 3:
-            tick(6 + pairs + part)
+            tick(7 + pairs + part)
     for one in gathers[first_down:first_pool]:
         one.ready()
     gain_two, shift_two = vec[10:11, :], vec[11:12, :]
@@ -811,7 +901,10 @@
     pieces = [g_down.at[:, :, pl.ds(many, few), :], g_down.at[:, :, pl.ds(0, many), :]]
     pieces += [g_up.at[:, :, :, pl.ds(half * 2 * width, 2 * width)] for half in (0, 1)]
     pieces += [w_up.at[:, :, :, pl.ds(at * width, width)] for at in (3, 0, 1, 2)]
-    scatters = [Scatter(place, ref, *recv[i], s_send.at[i], s_recv.at[i]) for i, ref in enumerate(pieces)]
+    scatters = [
+        (LineFirst if i == 0 else Scatter)(place, ref, *recv[i], s_send.at[i], s_recv.at[i])
+        for i, ref in enumerate(pieces)
+    ]
     down_a, down_b, up_a, up_b, of_mix, in_a, in_b, in_c = scatters
 
     for first_row, count, one in ((many, few, down_a), (0, many, down_b)):
@@ -848,10 +941,8 @@
         if part == 1:
             up_a.swap()
             down_b.to_first()
-            down_a.to_second()
         if part == 2:
             up_a.to_first()
-            down_a.to_line()
         if part == 3:
             up_b.swap()
             down_b.to_second()
@@ -873,7 +964,7 @@
                     down_b.to_line()
                 else:
                     up_a.to_second()
-                    down_a.to_plane()
+                    down_a.to_second()
 
     loop(2, through_up)
     norm_back(unit_one, inv_one, gain_one, 3, 4, 2, 128)
@@ -920,7 +1011,7 @@
         qkv[:, at[2]] = by_value.astype(BF16)
 
     after_pair = {
-        0: [down_b.to_plane],
+        0: [down_b.to_plane, down_a.to_line],
         1: [up_b.to_line, of_mix.to_second],
         2: [in_a.to_first, up_a.to_plane],
         3: [of_mix.to_line, in_a.to_second],
@@ -1048,8 +1139,8 @@
     sizes = [(few, width), (down_shard.shape[0] - few, width)] + [(block, 2 * width)] * 2 + [(block, width)] * 4
     scratch = [vmem((line, 2) + s.shape, BF16) for s in shards]
     scratch += [vmem((line, 2) + s.shape, BF16) for s in (down_shard, up_shard)]
-    for size in sizes:
-        scratch += Scatter.scratch(line, *size)
+    for i, size in enumerate(sizes):
+        scratch += (LineFirst if i == 0 else Scatter).scratch(line, *size)
     del scratch[-5]
     scratch += SmallSum.scratch(line, 24, width)
     scratch += [vmem((fsdp_size, 4, 16, width), BF16)]

time: 199 us -> 190 us (0.955); the launches traced: 197 us -> 190 us
  Pallas kernels: 195 us -> 188 us
    pallas_call x1, Pallas kernels: 189 us -> 182 us  [run_layer(): pl.pallas_call(functools.partial(layer_kernel, fsdp_size), out_shape=out_...]
where the time goes in v3:
time: 190 us
  Pallas kernels  188 us (99%)
  between operations  2.12 us (1%)
    pallas_call x1, Pallas kernels, run_layer(): pl.pallas_call(functools.partial(layer_kernel, fsdp_size), out_shape=out_...  182 us
    pallas_call x1, Pallas kernels, run_outputs(): pl.pallas_call(functools.partial(outputs_kernel, len(as_is), len(rounded)...  5.37 us

profile of v3, /device:TPU:8, one launch (start us, length us, event | category | flops | bytes accessed | tf_op | source)
XLA Modules:
  0.0 189.8 jit_solution(10187246541446368617)
XLA Ops:
  2.0 182.3 %layer.1 = (bf16[512,768]{1,0:T(8,128)(2,1)}, f32[512,768]{1,0:T(8,128)}, bf16[384,768]{1,0:T(8,128)(2,1)}, bf16[96,3072]{1,0:T(8,128)(2,1)}, bf16[96,768]{1,0:T...) custom-call(s32[1]{0:T(128)S(6)} %copy.38.refs_0_, s32[1]{0:T(128)S(6)} %copy.39.refs_1_, ...), custom_call_target="tpu_custom_call" | custom-call | tf_op jit(solution)/shard_map/layer/pallas_call | solution.py:1166
  184.2 5.4 %outputs.1 = (bf16[512,768]{1,0:T(8,128)(2,1)}, f32[512,768]{1,0:T(8,128)}, f32[96,768]{1,0:T(8,128)}, f32[96,2304]{1,0:T(8,128)}, f32[96,768]{1,0:T(8,128)}, /*...) custom-call(bf16[512,768]{1,0:T(8,128)(2,1)} %get-tuple-element.44.r, ...), custom_call_target="tpu_custom_call" | custom-call | tf_op jit(solution)/shard_map/outputs/pallas_call | solution.py:1219

commit v4 on v3

--- a/solution.py
+++ b/solution.py
@@ -554,7 +554,7 @@
 WHOLE = pl.BlockSpec(memory_space=pltpu.VMEM)
 SCALARS = pl.BlockSpec(memory_space=pltpu.SMEM)
 VMEM_BYTES = 67_043_328
-AHEAD = 4
+AHEAD = 2
 BF16, F32 = jnp.bfloat16, jnp.float32
 
 

time: 190 us -> 189 us (level)
  Pallas kernels: 188 us -> 186 us
where the time goes in v4:
time: 189 us
  Pallas kernels  186 us (98%)
  between operations  2.12 us (1%)
    pallas_call x1, Pallas kernels, run_layer(): pl.pallas_call(functools.partial(layer_kernel, fsdp_size), out_shape=out_...  181 us
    pallas_call x1, Pallas kernels, run_outputs(): pl.pallas_call(functools.partial(outputs_kernel, len(as_is), len(rounded)...  5.37 us

profile of v4, /device:TPU:8, one launch (start us, length us, event | category | flops | bytes accessed | tf_op | source)
XLA Modules:
  0.0 188.5 jit_solution(14996557502380993263)
XLA Ops:
  2.0 181.1 %layer.1 = (bf16[512,768]{1,0:T(8,128)(2,1)}, f32[512,768]{1,0:T(8,128)}, bf16[384,768]{1,0:T(8,128)(2,1)}, bf16[96,3072]{1,0:T(8,128)(2,1)}, bf16[96,768]{1,0:T...) custom-call(s32[1]{0:T(128)S(6)} %copy.38.refs_0_, s32[1]{0:T(128)S(6)} %copy.39.refs_1_, ...), custom_call_target="tpu_custom_call" | custom-call | tf_op jit(solution)/shard_map/layer/pallas_call | solution.py:1166
  183.0 5.4 %outputs.1 = (bf16[512,768]{1,0:T(8,128)(2,1)}, f32[512,768]{1,0:T(8,128)}, f32[96,768]{1,0:T(8,128)}, f32[96,2304]{1,0:T(8,128)}, f32[96,768]{1,0:T(8,128)}, /*...) custom-call(bf16[512,768]{1,0:T(8,128)(2,1)} %get-tuple-element.44.r, ...), custom_call_target="tpu_custom_call" | custom-call | tf_op jit(solution)/shard_map/outputs/pallas_call | solution.py:1219
